TPU v7x, 512 devices: a whole 4x4x16 slice. The times are simulated.
512 devices in a mesh: dp: 8 (over z_hi, core), ctx: 64 (over z_lo, y, x).
Axes of the slice: x: 4, y: 4, z: 16 (z_hi: 4, z_lo: 4; z = z_hi * 4 + z_lo), core: 2. Of those that a mesh axis runs over, the one named last changes fastest.
Arguments:
- pre_gate: bfloat16 [8, 8192, 2048], P('dp', 'ctx'), may hold values from -6 to 6
- post_gate: bfloat16 [8, 8192, 2048], P('dp', 'ctx'), may hold values from -6 to 6
- values: bfloat16 [8, 8192, 2048], P('dp', 'ctx'), may hold values from -6 to 6
- conv_out: bfloat16 [8, 8192, 2048], P('dp', 'ctx'), may hold values from -6 to 6
- grad_out: bfloat16 [8, 8192, 2048], P('dp', 'ctx'), may hold values from -6 to 6
- filter_param: bfloat16 [2048, 8192], P('ctx'), may hold values from -6 to 6
Outputs:
- d_pre_gate: bfloat16 [8, 8192, 2048], P('dp', 'ctx')
- d_post_gate: bfloat16 [8, 8192, 2048], P('dp', 'ctx')
- d_values: bfloat16 [8, 8192, 2048], P('dp', 'ctx')
- d_filter: float32 [2048, 8192], P(('ctx', 'dp'))
All inputs are finite; a program needn't handle non-finite values.
Results may differ from a plain program's by a relative error of at most 0.0058.
Values may be sent and summed in bfloat16 or wider, within the bound.
No kernel may reach another device: no remote copies, remote signals or barrier semaphores. Data moves between devices by JAX's collectives and lax.ppermute only.
A program may use at most 64 MiB of HBM per device.

v0:
```python
import math

import jax
import jax.numpy as jnp
from jax import lax
from jax.sharding import PartitionSpec as P

SECTION = 128


exact = lax.Precision.HIGHEST
full_turn = 2.0 * math.pi


def dft_tables(section, inner, whole):
    rows = jnp.arange(section, dtype=jnp.int32)
    half_rows = jnp.arange(section // 2, dtype=jnp.int32)
    columns = jnp.arange(inner, dtype=jnp.int32)
    first = (
        -full_turn / section * (rows[:, None] * half_rows[None, :] % section).astype(jnp.float32)
    )
    twist = -full_turn / whole * (rows[:, None] * columns[None, :] % whole).astype(jnp.float32)
    second = -full_turn / inner * (columns[:, None] * columns[None, :] % inner).astype(jnp.float32)
    first_cos = jnp.cos(first)
    first_sin = jnp.sin(first)
    second_cos = jnp.cos(second)
    second_sin = jnp.sin(second)
    single_table = jnp.concatenate([first_cos, first_sin], axis=0)
    paired_table = jnp.concatenate(
        [
            jnp.concatenate([first_cos, -first_sin], axis=1),
            jnp.concatenate([first_sin, first_cos], axis=1),
        ],
        axis=0,
    )
    later_forward = jnp.concatenate(
        [
            jnp.concatenate([second_cos, second_sin], axis=1),
            jnp.concatenate([-second_sin, second_cos], axis=1),
        ],
        axis=0,
    )
    later_inverse = jnp.concatenate(
        [
            jnp.concatenate([second_cos, -second_sin], axis=1),
            jnp.concatenate([second_sin, second_cos], axis=1),
        ],
        axis=0,
    )
    return (
        single_table,
        paired_table,
        jnp.cos(twist),
        jnp.sin(twist),
        later_forward,
        later_inverse,
    )


def forward(signal, tables, paired):
    single_table, paired_table, twist_cos, twist_sin, later_forward, later_inverse = tables
    table = paired_table if paired else single_table
    section_one = jnp.einsum("ja,cab->cjb", table, signal, precision=exact)
    count = twist_cos.shape[0]
    real_one = section_one[:, :count]
    imag_one = section_one[:, count:]
    joined = jnp.concatenate(
        [real_one * twist_cos - imag_one * twist_sin, real_one * twist_sin + imag_one * twist_cos],
        axis=2,
    )
    return jnp.einsum("ckb,bm->ckm", joined, later_forward, precision=exact)


def inverse(spectrum, tables):
    single_table, paired_table, twist_cos, twist_sin, later_forward, later_inverse = tables
    inner = twist_cos.shape[1]
    section_two = jnp.einsum("ckm,mb->ckb", spectrum, later_inverse, precision=exact)
    real_two = section_two[..., :inner]
    imag_two = section_two[..., inner:]
    stacked = jnp.concatenate(
        [real_two * twist_cos + imag_two * twist_sin, imag_two * twist_cos - real_two * twist_sin],
        axis=1,
    )
    scale = 1.0 / (twist_cos.shape[0] * inner)
    signal = jnp.einsum("ja,cjb->cab", paired_table, stacked, precision=exact) * scale
    channels = signal.shape[0]
    middle = signal.shape[1] // 2
    return (signal[:, :middle].reshape(channels, -1), signal[:, middle:].reshape(channels, -1))


def mirror(part):
    flipped = part[:, ::-1, ::-1]
    shifted = jnp.roll(flipped, 1, axis=1)
    zero_row = jnp.roll(part[:, 0, ::-1], 1, axis=1)
    return jnp.concatenate([zero_row[:, None], shifted[:, 1:]], axis=1)


def local(pre_gate, post_gate, values, conv_out, grad_out, filter_param):
    gate_rows = pre_gate[0].astype(jnp.float32)
    post_rows = post_gate[0].astype(jnp.float32)
    value_rows = values[0].astype(jnp.float32)
    grad_rows = grad_out[0].astype(jnp.float32)
    mixed = (gate_rows * value_rows).astype(jnp.bfloat16)
    grad_conv = (grad_rows * post_rows).astype(jnp.bfloat16)
    d_post = (grad_rows * conv_out[0].astype(jnp.float32)).astype(jnp.bfloat16)
    length = filter_param.shape[1]
    whole = 2 * length
    inner = whole // SECTION
    half_section = SECTION // 2
    tables = dft_tables(SECTION, inner, whole)
    kernel = (filter_param.astype(jnp.float32) * length ** (-0.5)).reshape(-1, half_section, inner)
    mixed_cols = mixed.T
    grad_cols = grad_conv.T
    mixed_chan, grad_chan = (
        lax.all_to_all(mixed_cols, "ctx", split_axis=0, concat_axis=1, tiled=True),
        lax.all_to_all(grad_cols, "ctx", split_axis=0, concat_axis=1, tiled=True),
    )
    kernel_spec = forward(kernel, tables, False)
    channels = mixed_chan.shape[0]
    both_signals = jnp.concatenate(
        [
            mixed_chan.reshape(channels, half_section, inner),
            grad_chan.reshape(channels, half_section, inner),
        ],
        axis=1,
    ).astype(jnp.float32)
    packed = forward(both_signals, tables, True)
    packed_real = packed[..., :inner]
    packed_imag = packed[..., inner:]
    mirror_real = mirror(packed_real)
    mirror_imag = mirror(packed_imag)
    mixed_real = 0.5 * (packed_real + mirror_real)
    mixed_imag = 0.5 * (packed_imag - mirror_imag)
    grad_real = 0.5 * (packed_imag + mirror_imag)
    grad_imag = 0.5 * (mirror_real - packed_real)
    kernel_real = kernel_spec[..., :inner]
    kernel_imag = kernel_spec[..., inner:]
    back_real = kernel_real * grad_real + kernel_imag * grad_imag
    back_imag = kernel_real * grad_imag - kernel_imag * grad_real
    factor = 1.0 / (lax.axis_size("dp") * math.sqrt(length))
    cross_real = (grad_real * mixed_real + grad_imag * mixed_imag) * factor
    cross_imag = (grad_imag * mixed_real - grad_real * mixed_imag) * factor
    joined = jnp.concatenate([back_real - cross_imag, back_imag + cross_real], axis=2)
    back_signal, terms = inverse(joined, tables)
    d_filter = lax.psum_scatter(terms, "dp", scatter_dimension=0, tiled=True)
    back_chan = back_signal.astype(jnp.bfloat16)
    back_rows = lax.all_to_all(back_chan, "ctx", split_axis=1, concat_axis=0, tiled=True).T.astype(
        jnp.float32
    )
    d_pre = (back_rows * value_rows).astype(jnp.bfloat16)
    d_val = (back_rows * gate_rows).astype(jnp.bfloat16)
    return (d_pre[None], d_post[None], d_val[None], d_filter)


def solution(mesh):
    return jax.shard_map(
        local,
        mesh=mesh,
        in_specs=(
            P("dp", "ctx", None),
            P("dp", "ctx", None),
            P("dp", "ctx", None),
            P("dp", "ctx", None),
            P("dp", "ctx", None),
            P("ctx", None),
        ),
        out_specs=(
            P("dp", "ctx", None),
            P("dp", "ctx", None),
            P("dp", "ctx", None),
            P(("ctx", "dp"), None),
        ),
        check_vma=False,
    )
```

profile of v0, /device:TPU:1, one launch (start us, length us, event | category | flops | bytes accessed | tf_op | source)
XLA Modules:
  0.0 267.7 jit_solution(14527157853922925956)
XLA Ops:
  7.2 1.3 copy.44
  8.5 0.0 copy-start.6
  8.5 1.4 copy.45
  9.9 0.0 copy-start.7
  9.9 0.9 fusion.21
  10.8 12.5 %all-to-all-start = ((bf16[64,32,128]{2,1,0:T(8,128)(2,1)}), bf16[64,32,128]{2,1,0:T(8,128)(2,1)S(1)}, u32[]{:S(2)}, u32[]{:S(2)}) async-start(bf16[64,32,128]{2,1,0:T(8,128)(2,1)} %bitcast.6), calls=%async_computation | async-start | bytes 1048576 | tf_op jit(solution)/shard_map/all_to_all | solution.py:115
  23.4 0.0 copy-done.6
  23.4 0.3 copy.47
  23.6 0.0 copy-done.7
  23.7 0.3 copy.48
  23.9 1.3 copy.58
  25.3 1.2 fusion.19
  26.5 13.9 %all-to-all-done = bf16[64,32,128]{2,1,0:T(8,128)(2,1)S(1)} async-done(((bf16[64,32,128]{2,1,0:T(8,128)(2,1)}), bf16[64,32,128]{2,1,0:T(8,128)(2,1)S(1)}, u32[]{:S(2)}, u32[]{:S(2)}) %all-to-all-start) | async-done | bytes 524320 | tf_op jit(solution)/shard_map/all_to_all | solution.py:115
  40.3 5.5 %all-to-all-start.1 = ((bf16[64,32,128]{2,1,0:T(8,128)(2,1)}), bf16[64,32,128]{2,1,0:T(8,128)(2,1)}, u32[]{:S(2)}, u32[]{:S(2)}) async-start(bf16[64,32,128]{2,1,0:T(8,128)(2,1)} %bitcast.10), calls=%async_computation.1 | async-start | bytes 1048576 | tf_op jit(solution)/shard_map/all_to_all | solution.py:116
  45.8 1.1 multiply_bitcast_fusion.1
  47.0 0.2 copy.70
  47.2 0.3 fusion.54
  47.4 0.1 copy.41
  47.5 0.3 fusion.53
  47.8 0.1 copy.42
  47.9 0.8 fusion.61
  48.6 0.1 fusion.59
  48.8 0.3 fusion.58
  49.1 0.3 fusion.51
  49.3 5.0 %convolution_bitcast_fusion.1 = f32[32,256,128]{1,2,0:T(8,128)} fusion(f32[32,64,128]{2,1,0:T(8,128)S(1)} %bitcast.69, f32[128,64]{0,1:T(8,128)S(1)} %get-tuple-element.30, f32[128,64]{0,1:T(8,128)S(1)} %get-tuple-element.31), kind=kOutput, calls=%fused_computation.17 | convolution fusion | flops 805322752 | bytes 5308416 | tf_op jit(solution)/shard_map/ja,cab->cjb/dot_general | solution.py:63
  54.4 0.7 copy.46
  55.1 6.3 %all-to-all-done.1 = bf16[64,32,128]{2,1,0:T(8,128)(2,1)} async-done(((bf16[64,32,128]{2,1,0:T(8,128)(2,1)}), bf16[64,32,128]{2,1,0:T(8,128)(2,1)}, u32[]{:S(2)}, u32[]{:S(2)}) %all-to-all-start.1) | async-done | bytes 524320 | tf_op jit(solution)/shard_map/all_to_all | solution.py:116
  61.4 1.7 copy.49
  63.1 2.8 %convolution_bitcast_fusion = f32[32,256,128]{1,2,0:T(8,128)S(1)} fusion(bf16[32,64,128]{1,2,0:T(8,128)(2,1)S(1)} %bitcast.66, bf16[32,64,128]{1,2,0:T(8,128)(2,1)S(1)} %bitcast.65, f32[128,64]{0,1:T(8,128)S(1)} %get-tuple-element.31, f32[128,64]{0,1:T(8,128)S(1)} %get-tuple-element.30, f32[128,64]{0,1:T(8,128)} %fusion.61), kind=kOutput, calls=%fused_computation.16 | convolution fusion | flops 1612808192 | bytes 5341184 | tf_op jit(solution)/shard_map/ja,cab->cjb/dot_general | solution.py:63
  65.9 2.9 %multiply_subtract_fusion.2 = (f32[32,128,128]{1,2,0:T(8,128)S(1)}, f32[32,128,128]{1,2,0:T(8,128)S(1)}, f32[32,128,128]{1,2,0:T(8,128)}, f32[32,128,128]{1,2,0:T(8,128)}) fusion(f32[32,256,128]{1,2,0:T(8,128)S(1)} %convolution_bitcast_fusion, f32[128,128]{0,1:T(8,128)S(1)} %copy.42, f32[128,128]{0,1:T(8,128)S(1)} %copy.41, f32[32,256,128]{1,2,0:T(8,128)S(1)} %copy-done.2), kind=kLoop, calls=%fused_computation.30 | loop fusion | flops 6291456 | bytes 16908288 | tf_op jit(solution)/shard_map/sub | solution.py:68
  68.8 7.1 %fusion.4 = f32[32,128,256]{2,1,0:T(8,128)S(1)} fusion(f32[32,128,128]{1,2,0:T(8,128)S(1)} %get-tuple-element.17, f32[32,128,128]{1,2,0:T(8,128)S(1)} %get-tuple-element.16, f32[128,128]{1,0:T(8,128)S(1)} %get-tuple-element.33, f32[128,128]{1,0:T(8,128)S(1)} %fusion.58, f32[128,128]{1,0:T(8,128)S(1)} %get-tuple-element.32), kind=kOutput, calls=%fused_computation.4 | convolution fusion | flops 3222470656 | bytes 8585216 | tf_op jit(solution)/shard_map/ckb,bm->ckm/dot_general | solution.py:71
  76.0 0.7 fusion.69
  76.7 1.9 fusion.70
  78.6 0.0 copy-done
  78.6 0.8 rev.9
  79.4 0.7 slice.115
  80.1 1.4 rev.8
  81.5 1.4 slice.110
  82.9 17.7 %slice.91 = f32[32,127,128]{2,1,0:T(8,128)} reverse(f32[32,127,128]{2,1,0:T(8,128)} %get-tuple-element.23), dimensions={1,2} | reverse | bytes 4161536 | tf_op jit(solution)/shard_map/jit(_roll_static)/slice | solution.py:93
  100.6 11.9 %slice.97 = f32[32,127,128]{2,1,0:T(8,128)} reverse(f32[32,127,128]{2,1,0:T(8,128)S(1)} %get-tuple-element.22), dimensions={1,2} | reverse | bytes 4161536 | tf_op jit(solution)/shard_map/jit(_roll_static)/slice | solution.py:93
  112.5 0.8 pad_maximum_fusion.8
  113.3 0.8 pad_maximum_fusion.7
  114.1 8.8 %fusion = f32[32,128,256]{2,1,0:T(8,128)S(1)} fusion(f32[32,128,128]{1,2,0:T(8,128)} %get-tuple-element.28, f32[32,128,128]{1,2,0:T(8,128)} %get-tuple-element.29, f32[128,128]{1,0:T(8,128)S(1)} %get-tuple-element.33, f32[128,128]{1,0:T(8,128)S(1)} %fusion.58, f32[128,128]{1,0:T(8,128)S(1)} %get-tuple-element.32), kind=kOutput, calls=%fused_computation | convolution fusion | flops 3222470656 | bytes 8585216 | tf_op jit(solution)/shard_map/ckb,bm->ckm/dot_general | solution.py:71
  123.0 2.2 multiply_subtract_fusion.1
  125.1 4.0 %fusion.8 = f32[32,128,256]{1,2,0:T(8,128)S(1)} fusion(f32[32,128,128]{2,1,0:T(8,128)S(1)} %get-tuple-element.13, f32[32,128,128]{2,1,0:T(8,128)S(1)} %get-tuple-element.12, f32[128,128]{1,0:T(8,128)S(1)} %get-tuple-element.33, f32[128,128]{1,0:T(8,128)S(1)} %get-tuple-element.32, f32[128,128]{1,0:T(8,128)S(1)} %fusion.58), kind=kOutput, calls=%fused_computation.8 | convolution fusion | flops 3222470656 | bytes 8585216 | tf_op jit(solution)/shard_map/ckm,mb->ckb/dot_general | solution.py:77
  129.1 0.0 copy-start.8
  129.1 0.8 multiply_add_fusion
  130.0 4.5 %multiply_bitcast_fusion = f32[32,128,128]{2,1,0:T(8,128)S(1)} fusion(f32[32,128,128]{1,2,0:T(8,128)S(1)} %get-tuple-element.15, f32[32,128,128]{1,2,0:T(8,128)S(1)} %get-tuple-element.14, f32[128,64]{0,1:T(8,128)S(1)} %get-tuple-element.31, f32[128,64]{0,1:T(8,128)S(1)} %get-tuple-element.30, f32[128,64]{0,1:T(8,128)S(1)} %copy-done.8), kind=kOutput, calls=%fused_computation.20 | convolution fusion | flops 1612283904 | bytes 6389760 | tf_op jit(solution)/shard_map/ja,cjb->cab/dot_general | solution.py:85
  134.5 0.1 slice.160
  134.6 1.1 copy.57
  135.7 6.6 %all-to-all-start.2 = ((bf16[32,64,128]{2,0,1:T(8,128)(2,1)}), bf16[32,64,128]{2,0,1:T(8,128)(2,1)}, u32[]{:S(2)}, u32[]{:S(2)}) async-start(bf16[32,64,128]{2,0,1:T(8,128)(2,1)} %copy.57), calls=%async_computation.2 | async-start | bytes 1048576 | tf_op jit(solution)/shard_map/all_to_all | solution.py:147
  142.3 0.0 all-reduce.3.cloned.1.call-start
  142.4 0.1 slice.122
  142.4 0.0 copy-start.5
  142.5 1.6 copy.73
  144.0 0.0 all-reduce.3.cloned.1.call-update
  144.1 1.0 copy.60
  145.1 1.3 dynamic-slice
  147.0 108.9 %all-reduce.3.cloned.1.call-done = f32[32,8192]{1,0:T(8,128)} async-done(((f32[32,8192]{1,0:T(8,128)}), f32[32,8192]{1,0:T(8,128)}) %all-reduce.3.cloned.1.call-update) | async-done | bytes 1048592
  255.9 1.6 constant_dynamic-slice_fusion
  257.5 0.0 all-to-all-done.2
  257.5 1.3 fusion.20
  258.8 1.0 copy.59
  259.8 1.0 copy.61
  (11 shorter events, 0.0 us)
Async XLA Ops:
  8.5 14.9 %copy-start.6 = (bf16[1,128,2048]{2,1,0:T(8,128)(2,1)S(1)}, bf16[1,128,2048]{2,1,0:T(8,128)(2,1)}, u32[]{:S(2)}) copy-start(bf16[1,128,2048]{2,1,0:T(8,128)(2,1)} %param.10) | copy-start | bytes 1572868
  9.9 13.8 %copy-start.7 = (bf16[1,128,2048]{2,1,0:T(8,128)(2,1)S(1)}, bf16[1,128,2048]{2,1,0:T(8,128)(2,1)}, u32[]{:S(2)}) copy-start(bf16[1,128,2048]{2,1,0:T(8,128)(2,1)} %param.7) | copy-start | bytes 1572868
  10.8 29.5 %all-to-all-start = ((bf16[64,32,128]{2,1,0:T(8,128)(2,1)}), bf16[64,32,128]{2,1,0:T(8,128)(2,1)S(1)}, u32[]{:S(2)}, u32[]{:S(2)}) async-start(bf16[64,32,128]{2,1,0:T(8,128)(2,1)} %bitcast.6), calls=%async_computation | async-start | bytes 1048576 | tf_op jit(solution)/shard_map/all_to_all | solution.py:115
  40.3 21.1 %all-to-all-start.1 = ((bf16[64,32,128]{2,1,0:T(8,128)(2,1)}), bf16[64,32,128]{2,1,0:T(8,128)(2,1)}, u32[]{:S(2)}, u32[]{:S(2)}) async-start(bf16[64,32,128]{2,1,0:T(8,128)(2,1)} %bitcast.10), calls=%async_computation.1 | async-start | bytes 1048576 | tf_op jit(solution)/shard_map/all_to_all | solution.py:116
  63.1 2.8 %copy-start.2 = (f32[32,256,128]{1,2,0:T(8,128)S(1)}, f32[32,256,128]{1,2,0:T(8,128)}, u32[]{:S(2)}) copy-start(f32[32,256,128]{1,2,0:T(8,128)} %convolution_bitcast_fusion.1) | copy-start | bytes 12582916
  76.0 2.7 copy-start
  114.1 8.9 %copy-start.1 = (f32[32,128,256]{2,1,0:T(8,128)S(1)}, f32[32,128,256]{2,1,0:T(8,128)}, u32[]{:S(2)}) copy-start(f32[32,128,256]{2,1,0:T(8,128)} %copy-done) | copy-start | bytes 12582916
  114.1 8.9 %copy-start.3 = (f32[32,127,128]{2,1,0:T(8,128)S(1)}, f32[32,127,128]{2,1,0:T(8,128)}, u32[]{:S(2)}) copy-start(f32[32,127,128]{2,1,0:T(8,128)} %slice.91) | copy-start | bytes 6242308
  114.1 8.9 %copy-start.4 = (f32[32,127,128]{2,1,0:T(8,128)S(1)}, f32[32,127,128]{2,1,0:T(8,128)}, u32[]{:S(2)}) copy-start(f32[32,127,128]{2,1,0:T(8,128)} %slice.97) | copy-start | bytes 6242308
  129.1 0.9 copy-start.8
  135.7 121.8 %all-to-all-start.2 = ((bf16[32,64,128]{2,0,1:T(8,128)(2,1)}), bf16[32,64,128]{2,0,1:T(8,128)(2,1)}, u32[]{:S(2)}, u32[]{:S(2)}) async-start(bf16[32,64,128]{2,0,1:T(8,128)(2,1)} %copy.57), calls=%async_computation.2 | async-start | bytes 1048576 | tf_op jit(solution)/shard_map/all_to_all | solution.py:147
  142.3 113.6 %all-reduce.3.cloned.1.call-start = ((), (), s32[]{:S(2)}) async-start(), calls=%async_computation.3 | async-start | bytes 2097152
  142.4 1.6 copy-start.5
Sparse Core Ops, SparseCore 0:
  146.1 109.7 all-reduce.2
where the time goes:
time: 270 us; the launch traced here: 268 us
  waiting for transfers between devices  129 us (48%)
  local copies, waits for them, and re-layouts  52.6 us (19%)
  matrix products  32.2 us (12%)
  starting transfers between devices  24.7 us (9%)
  between operations  15 us (6%)
  other arithmetic  14.1 us (5%)
    unnamed x2, waiting for transfers between devices  109 us
    slice x3, local copies, waits for them, and re-layouts, mirror(): shifted = jnp.roll(flipped, 1, axis=1)  31.5 us
    dot_general x2, matrix products, forward(): return jnp.einsum('ckb,bm->ckm', joined, later_forward, precision=exact)  16 us
    all_to_all x1, waiting for transfers between devices, local(): lax.all_to_all(mixed_cols, 'ctx', split_axis=0, concat_axis=1, tiled=True)  13.9 us
    all_to_all x1, starting transfers between devices, local(): lax.all_to_all(mixed_cols, 'ctx', split_axis=0, concat_axis=1, tiled=True)  12.5 us
    unnamed x30, local copies, waits for them, and re-layouts  12.3 us
    dot_general x2, matrix products, forward(): section_one = jnp.einsum('ja,cab->cjb', table, signal, precision=exact)  7.79 us
    all_to_all x1, starting transfers between devices, local(): lax.all_to_all(back_chan, 'ctx', split_axis=1, concat_axis=0, tiled=True)  6.6 us
  transfers between devices with their start and end apart: 4, of which 3 were waited for; matrix products, arithmetic and copies ran while one was open for 7% of the time, Pallas kernels for 0%

commit v1 on v0

v1 whole, which is shorter than its diff:
```python
import functools

import jax
import jax.numpy as jnp
from jax import lax
from jax.experimental import pallas as pl
from jax.experimental.pallas import tpu as pltpu
from jax.sharding import Mesh
from jax.sharding import PartitionSpec as P


L = 128
R = 64
CH = 32
DP = ("zh", "core")
CTX = ("zl", "y", "x")
F32 = jnp.float32
BF16 = jnp.bfloat16
VMEM_LIMIT = 10 << 20
GROUPS = ((0, 1), (2, 3))


def pre_body(x_ref, y_ref, send_ref):
    width = x_ref.shape[1]
    product = (x_ref[...].astype(F32) * y_ref[...].astype(F32)).astype(BF16)
    send_ref[...] = product.T.reshape(width // CH, CH, L)


def pre(x, y):
    channels = x.shape[1]
    width = 512
    block = pl.BlockSpec((L, width), lambda i: (0, i))
    return pl.pallas_call(
        pre_body,
        grid=(channels // width,),
        in_specs=[block] * 2,
        out_specs=pl.BlockSpec((width // CH, CH, L), lambda i: (i, 0, 0)),
        out_shape=jax.ShapeDtypeStruct((channels // CH, CH, L), BF16),
        cost_estimate=pl.CostEstimate(flops=0, bytes_accessed=3 * channels * L * 2, transcendentals=0),
    )(x, y)


def post_body(back_ref, gate_ref, value_ref, d_pre_ref, d_val_ref):
    width = gate_ref.shape[1]
    back = back_ref[...].reshape(width, L).T.astype(F32)
    d_pre_ref[...] = (back * value_ref[...].astype(F32)).astype(BF16)
    d_val_ref[...] = (back * gate_ref[...].astype(F32)).astype(BF16)


def post(back, gate, value):
    channels = gate.shape[1]
    width = 512
    block = pl.BlockSpec((L, width), lambda i: (0, i))
    shape = jax.ShapeDtypeStruct((L, channels), BF16)
    return pl.pallas_call(
        post_body,
        grid=(channels // width,),
        in_specs=[pl.BlockSpec((width // CH, CH, L), lambda i: (i, 0, 0)), block, block],
        out_specs=(block, block),
        out_shape=(shape, shape),
        cost_estimate=pl.CostEstimate(flops=0, bytes_accessed=5 * channels * L * 2, transcendentals=0),
        compiler_params=pltpu.CompilerParams(vmem_limit_bytes=VMEM_LIMIT),
        name="post",
    )(back, gate, value)


def widen(recv_ref, wide):
    def rows(r, _):
        at = pl.multiple_of(r * 8, 8)
        for c in range(0, CH, 16):
            x = recv_ref[pl.ds(at, 8), c : c + 16, :].astype(F32)
            wide[c : c + 16, pl.ds(at, 8), :] = jnp.swapaxes(x, 0, 1)
        return 0

    lax.fori_loop(0, R // 8, rows, 0)


def narrow(wide, send_ref):
    def rows(r, _):
        at = pl.multiple_of(r * 8, 8)
        for c in range(0, CH, 16):
            x = jnp.swapaxes(wide[c : c + 16, pl.ds(at, 8), :], 0, 1)
            send_ref[pl.ds(at, 8), c : c + 16, :] = x.astype(BF16)
        return 0

    lax.fori_loop(0, R // 8, rows, 0)


def correlate(count, load_grad, load_other, store, halves):
    lane8 = lax.broadcasted_iota(jnp.int32, (8, L), 1)
    sub8 = lax.broadcasted_iota(jnp.int32, (8, L), 0)
    lane16 = lax.broadcasted_iota(jnp.int32, (16, L), 1)
    row16 = lax.broadcasted_iota(jnp.int32, (16, L), 0)
    lane = lax.broadcasted_iota(jnp.int32, (R, L), 1)
    for gp, vp, w, rhs, acc in halves:
        gp[pl.ds(R, 8), :] = jnp.zeros((8, L), F32)
        vp[pl.ds(0, 8), :] = jnp.zeros((8, L), F32)
        w[pl.ds(4, 1)] = jnp.zeros((1, 128, L), BF16)

    def build(c, half):
        gp, vp, w, rhs, _ = halves[half]
        gp[pl.ds(0, R), :] = load_grad(c)
        vp[pl.ds(8, R), :] = load_other(c)
        rows = gp[pl.ds(0, R), :]
        following = gp[pl.ds(1, R), :]
        for u in range(8):
            x = rows
            if u:
                x = pltpu.roll(jnp.where(lane >= 16 * u, rows, following), L - 16 * u, 1)
            x = x.astype(BF16)
            for t in range(4):
                w[t, pl.ds(16 * u, 16), :] = x[16 * t : 16 * t + 16]
        for j in range(R):
            h, i = divmod(j, 16)
            here = vp[pl.ds(8 + j, 8, stride=0), :]
            before = vp[pl.ds(7 + j, 8, stride=0), :]
            shifted = [
                pltpu.roll(jnp.where(lane8 < L - 8 * p - sub8, here, before), 8 * p, 1, stride=1, stride_axis=0)
                for p in range(2)
            ]
            rhs[h, pl.ds(16 * i, 16), :] = jnp.concatenate(shifted, axis=0).astype(BF16)

    def multiply(half):
        _, _, w, rhs, acc = halves[half]
        for group in GROUPS:
            depth = 4 - group[0]
            lhs = jnp.concatenate(
                [jnp.concatenate([w[min(p + h, 4)] for h in range(depth)], axis=1) for p in group], axis=0
            )
            cols = jnp.concatenate([rhs[h] for h in range(depth)], axis=1)
            out = lax.dot_general(lhs, cols, (((1,), (1,)), ((), ())), preferred_element_type=F32)
            for n, p in enumerate(group):
                acc[0, p] = out[128 * n : 128 * n + 128, :L]
                acc[1, p] = out[128 * n : 128 * n + 128, L:]

    def finish(c, half):
        _, _, _, _, acc = halves[half]
        tops = []
        for u in range(8):
            lo, hi = ([acc[k, p, pl.ds(16 * u, 16), :] for p in range(4)] for k in range(2))
            lo[0] = jnp.where(row16 >= lane16 // 16, lo[0], 0.0)
            hi[0] = jnp.where(row16 >= lane16 // 16 + 8, hi[0], 0.0)
            hi = jnp.concatenate(hi, axis=0)
            tops.append(jnp.concatenate(lo, axis=0) + jnp.concatenate([hi[8:], hi[:8]], axis=0))

        def pair(p, q, width):
            low = (lane & width) == 0
            a = jnp.where(low, p, q)
            b = jnp.where(low, q, p)
            right = pltpu.roll(b, width, 1)
            left = right if 2 * width == L else pltpu.roll(b, L - width, 1)
            return jnp.where(low, a, right) + pltpu.roll(jnp.where(low, left, a), R - width // 16, 0)

        fours = [pair(tops[u], tops[u + 4], 64) for u in range(4)]
        twos = [pair(fours[u], fours[u + 2], 32) for u in range(2)]
        store(c, pair(twos[0], twos[1], 16))

    build(0, 0)

    def step(n, _):
        c = 2 * n
        multiply(0)
        build(c + 1, 1)
        finish(jnp.maximum(c - 1, 0), 1)
        multiply(1)
        build(jnp.minimum(c + 2, count - 1), 0)
        finish(c, 0)
        return 0

    lax.fori_loop(0, count // 2, step, 0)
    finish(count - 1, 1)


HALF = [
    pltpu.VMEM((R + 8, L), F32),
    pltpu.VMEM((R + 8, L), F32),
    pltpu.VMEM((5, 128, L), BF16),
    pltpu.VMEM((4, 256, L), BF16),
    pltpu.VMEM((2, 4, 128, L), F32),
]
WHOLE = pl.BlockSpec(memory_space=pltpu.VMEM)
CONV_COST = pl.CostEstimate(flops=CH * 512 * 512 * 256 * 2, bytes_accessed=2 << 20, transcendentals=0)


def back_body(recv_ref, taps_ref, send_ref, grad_ref, wide, flat, *bufs, scale):
    widen(recv_ref, wide)

    def load_grad(c):
        rows = wide[c]
        grad_ref[c] = rows.astype(BF16)
        return rows

    def store(c, rows):
        flat[c] = rows * scale

    correlate(CH, load_grad, lambda c: taps_ref[c].astype(F32), store, (bufs[:5], bufs[5:]))
    narrow(flat, send_ref)


def conv_back(recv, taps, scale):
    return pl.pallas_call(
        functools.partial(back_body, scale=scale),
        in_specs=[WHOLE] * 2,
        out_specs=(WHOLE, WHOLE),
        out_shape=(jax.ShapeDtypeStruct((R, CH, L), BF16), jax.ShapeDtypeStruct((CH, R, L), BF16)),
        scratch_shapes=[pltpu.VMEM((CH, R, L), F32)] * 2 + HALF * 2,
        cost_estimate=CONV_COST,
        compiler_params=pltpu.CompilerParams(vmem_limit_bytes=VMEM_LIMIT),
        name="conv_back",
    )(recv, taps)


def channel_of(n, core):
    return lax.div(n, 4) * 8 + core * 4 + lax.rem(n, 4)


def term_first_body(core_ref, recv_ref, grad_ref, term_ref, mixed_ref, wide, *bufs, scale):
    widen(recv_ref, wide)

    def narrow_rows(c, _):
        mixed_ref[c] = wide[c].astype(BF16)
        return 0

    lax.fori_loop(0, CH, narrow_rows, 0)
    core = core_ref[0]

    def store(n, rows):
        term_ref[n] = rows * scale

    correlate(
        CH // 2,
        lambda n: grad_ref[channel_of(n, core)].astype(F32),
        lambda n: wide[channel_of(n, core)],
        store,
        (bufs[:5], bufs[5:]),
    )


def term_second_body(core_ref, mixed_ref, grad_ref, term_ref, *bufs, scale):
    core = core_ref[0]

    def store(n, rows):
        term_ref[n] = rows * scale

    correlate(
        CH // 2,
        lambda n: grad_ref[channel_of(n, core)].astype(F32),
        lambda n: mixed_ref[channel_of(n, core)].astype(F32),
        store,
        (bufs[:5], bufs[5:]),
    )


def conv_term(body, core, mixed, grad, scale, wide):
    rows = jax.ShapeDtypeStruct((CH, R, L), BF16)
    terms = jax.ShapeDtypeStruct((CH // 2, R, L), F32)
    return pl.pallas_call(
        functools.partial(body, scale=scale),
        in_specs=[pl.BlockSpec(memory_space=pltpu.SMEM)] + [WHOLE] * 2,
        out_specs=(WHOLE, WHOLE) if wide else WHOLE,
        out_shape=(terms, rows) if wide else terms,
        scratch_shapes=([pltpu.VMEM((CH, R, L), F32)] if wide else []) + HALF * 2,
        cost_estimate=CONV_COST,
        compiler_params=pltpu.CompilerParams(vmem_limit_bytes=VMEM_LIMIT),
    )(core, mixed, grad)


def sum_over_zh(both):
    zh = lax.axis_index("zh")
    count = lax.axis_size("zh")
    pick = functools.partial(lax.dynamic_index_in_dim, axis=0, keepdims=False)
    parts = []
    for shift in (2, 1, 3):
        ahead = [(i, (i + shift) % count) for i in range(count)]
        parts.append(lax.ppermute(pick(both, (zh + shift) % count).astype(BF16), "zh", ahead))
    return pick(both, zh) + (parts[0].astype(F32) + (parts[1].astype(F32) + parts[2].astype(F32)))


def local(pre_gate, post_gate, values, conv_out, grad_out, filter_param):
    gate, value, grad = pre_gate[0], values[0], grad_out[0]
    length = filter_param.shape[1]
    exchange = functools.partial(lax.all_to_all, axis_name=CTX, split_axis=0, concat_axis=0, tiled=True)
    grad_send = pre(grad, post_gate[0])
    grad_chan = exchange(grad_send)
    mixed_send = pre(gate, value)
    d_post = (grad.astype(F32) * conv_out[0].astype(F32)).astype(BF16)
    taps = filter_param.reshape(CH, R, L)
    mixed_chan = exchange(mixed_send)
    scale = length ** (-0.5)
    batch = lax.axis_size("zh") * lax.axis_size("core")
    back, grad_rows = conv_back(grad_chan, taps, scale)
    back = exchange(back)
    core = lax.axis_index("core").astype(jnp.int32)
    scale = scale / batch
    terms, mixed_rows = conv_term(term_first_body, (1 - core).reshape(1), mixed_chan, grad_rows, scale, True)
    terms = lax.ppermute(terms, "core", [(0, 1), (1, 0)])
    own = conv_term(term_second_body, core.reshape(1), mixed_rows, grad_rows, scale, False)
    d_filter = sum_over_zh((own + terms).reshape(4, 4, R, L)).reshape(4, length)
    d_pre, d_val = post(back, gate, value)
    return (d_pre[None], d_post[None], d_val[None], d_filter)


def solution(mesh):
    fine = Mesh(mesh.devices.reshape(4, 2, 4, 4, 4), DP + CTX)
    tokens = P(DP, CTX, None)
    return jax.shard_map(
        local,
        mesh=fine,
        in_specs=(tokens,) * 5 + (P(CTX, None),),
        out_specs=(tokens, tokens, tokens, P(CTX + DP, None)),
        check_vma=False,
    )
```

time: 270 us -> 113 us (0.42)
  the two profiles are of different devices: /device:TPU:1 before, /device:TPU:24 now
where the time goes in v1:
time: 113 us; the launch traced here: 112 us
  starting transfers between devices  52.9 us (47%)
  Pallas kernels  34.6 us (31%)
  waiting for transfers between devices  21.7 us (19%)
    ppermute x3, starting transfers between devices, sum_over_zh(): lax.ppermute(pick(both, (zh + shift) % count).astype(BF16), 'zh', ahead)  22.9 us
    pallas_call x1, Pallas kernels, conv_back(): pl.pallas_call(functools.partial(back_body, scale=scale), in_specs=[WHOLE...  13.1 us
    pallas_call x2, Pallas kernels, conv_term(): pl.pallas_call(functools.partial(body, scale=scale), in_specs=[pl.BlockSp...  12.8 us
    all_to_all x1, waiting for transfers between devices, local(): grad_chan = exchange(grad_send)  12.2 us
    all_to_all x1, starting transfers between devices, local(): grad_chan = exchange(grad_send)  11.8 us
    all_to_all x1, starting transfers between devices, local(): back = exchange(back)  9.03 us
    ppermute x3, waiting for transfers between devices, sum_over_zh(): lax.ppermute(pick(both, (zh + shift) % count).astype(BF16), 'zh', ahead)  7.79 us
    all_to_all x1, starting transfers between devices, local(): mixed_chan = exchange(mixed_send)  7.28 us
  transfers between devices with their start and end apart: 7, of which 4 were waited for; matrix products, arithmetic and copies ran while one was open for 2% of the time, Pallas kernels for 26%

profile of v1, /device:TPU:24, one launch (start us, length us, event | category | flops | bytes accessed | tf_op | source)
XLA Modules:
  0.0 112.0 jit_solution(8209014883139594013)
XLA Ops:
  0.6 3.5 %shard_map.93 = bf16[64,32,128]{2,1,0:T(8,128)(2,1)} custom-call(bf16[128,2048]{1,0:T(8,128)(2,1)} %bitcast.31, bf16[128,2048]{1,0:T(8,128)(2,1)} %bitcast.34), custom_call_target="tpu_custom_call" | custom-call | bytes 1572864 | tf_op jit(solution)/shard_map/pallas_call | solution.py:33
  4.1 11.8 %all-to-all-start = ((bf16[64,32,128]{2,1,0:T(8,128)(2,1)}), bf16[64,32,128]{2,1,0:T(8,128)(2,1)S(1)}, u32[]{:S(2)}, u32[]{:S(2)}) async-start(bf16[64,32,128]{2,1,0:T(8,128)(2,1)} %shard_map.93), calls=%async_computation | async-start | bytes 1048576 | tf_op jit(solution)/shard_map/all_to_all | solution.py:284
  15.9 3.5 %shard_map.94 = bf16[64,32,128]{2,1,0:T(8,128)(2,1)} custom-call(bf16[128,2048]{1,0:T(8,128)(2,1)} %bitcast.26, bf16[128,2048]{1,0:T(8,128)(2,1)} %bitcast.28), custom_call_target="tpu_custom_call" | custom-call | bytes 1572864 | tf_op jit(solution)/shard_map/pallas_call | solution.py:33
  19.4 0.0 copy-start.4
  19.4 12.2 %all-to-all-done.recv_ref = bf16[64,32,128]{2,1,0:T(8,128)(2,1)S(1)} async-done(((bf16[64,32,128]{2,1,0:T(8,128)(2,1)}), bf16[64,32,128]{2,1,0:T(8,128)(2,1)S(1)}, u32[]{:S(2)}, u32[]{:S(2)}) %all-to-all-start) | async-done | bytes 524320 | tf_op jit(solution)/shard_map/all_to_all | solution.py:284
  31.5 7.3 %all-to-all-start.2 = ((bf16[64,32,128]{2,1,0:T(8,128)(2,1)}), bf16[64,32,128]{2,1,0:T(8,128)(2,1)S(1)}, u32[]{:S(2)}, u32[]{:S(2)}) async-start(bf16[64,32,128]{2,1,0:T(8,128)(2,1)} %shard_map.94), calls=%async_computation.2 | async-start | bytes 1048576 | tf_op jit(solution)/shard_map/all_to_all | solution.py:288
  38.8 0.0 copy-done.4
  38.8 0.1 copy.10
  38.9 13.1 %conv_back.1 = (bf16[64,32,128]{2,1,0:T(8,128)(2,1)}, bf16[32,64,128]{2,1,0:T(8,128)(2,1)S(1)}) custom-call(bf16[64,32,128]{2,1,0:T(8,128)(2,1)S(1)} %all-to-all-done.recv_ref, bf16[32,64,128]{2,1,0:T(8,128)(2,1)S(1)} %bitcast.30), custom_call_target="tpu_custom_call" | custom-call | flops 4294967296 | bytes 2097152 | tf_op jit(solution)/shard_map/conv_back/pallas_call | solution.py:201
  52.0 1.7 %all-to-all-done.2.recv_ref = bf16[64,32,128]{2,1,0:T(8,128)(2,1)S(1)} async-done(((bf16[64,32,128]{2,1,0:T(8,128)(2,1)}), bf16[64,32,128]{2,1,0:T(8,128)(2,1)S(1)}, u32[]{:S(2)}, u32[]{:S(2)}) %all-to-all-start.2) | async-done | bytes 524320 | tf_op jit(solution)/shard_map/all_to_all | solution.py:288
  53.7 9.0 %all-to-all-start.1 = ((bf16[64,32,128]{2,1,0:T(8,128)(2,1)}), bf16[64,32,128]{2,1,0:T(8,128)(2,1)S(1)}, u32[]{:S(2)}, u32[]{:S(2)}) async-start(bf16[64,32,128]{2,1,0:T(8,128)(2,1)} %get-tuple-element.10), calls=%async_computation.1 | async-start | bytes 1048576 | tf_op jit(solution)/shard_map/all_to_all | solution.py:292
  62.8 6.6 %shard_map.95 = (f32[16,64,128]{2,1,0:T(8,128)S(1)}, bf16[32,64,128]{2,1,0:T(8,128)(2,1)S(1)}) custom-call(s32[1]{0:T(128)} %bitcast.7.core_ref, bf16[64,32,128]{2,1,0:T(8,128)(2,1)S(1)} %all-to-all-done.2.recv_ref, bf16[32,64,128]{2,1,0:T(8,128)(2,1)S(1)} %get-tuple-element.13.grad_ref), custom_call_target="tpu_custom_call" | custom-call | flops 4294967296 | bytes 2097152 | tf_op jit(solution)/shard_map/pallas_call | solution.py:257
  69.3 1.9 %collective-permute-start = (f32[16,64,128]{2,1,0:T(8,128)S(1)}, f32[16,64,128]{2,1,0:T(8,128)S(1)}, u32[]{:S(2)}, u32[]{:S(2)}) collective-permute-start(f32[16,64,128]{2,1,0:T(8,128)S(1)} %get-tuple-element.15), channel_id=1, source_target_pairs={{0,64},{64,0},{1,65},{65,1},{2,66},{66,2},{3,67},{67,3},{4,68},{68... | collective-permute-start | bytes 1572872 | tf_op jit(solution)/shard_map/ppermute | solution.py:296
  71.3 6.2 %shard_map.96 = f32[16,64,128]{2,1,0:T(8,128)S(1)} custom-call(s32[1]{0:T(128)} %bitcast.6.core_ref, bf16[32,64,128]{2,1,0:T(8,128)(2,1)S(1)} %get-tuple-element.14.mixed_ref, bf16[32,64,128]{2,1,0:T(8,128)(2,1)S(1)} %get-tuple-element.13.grad_ref), custom_call_target="tpu_custom_call" | custom-call | flops 4294967296 | bytes 2097152 | tf_op jit(solution)/shard_map/pallas_call | solution.py:257
  77.5 0.0 collective-permute-done
  77.5 0.0 copy-start.2
  77.5 0.0 copy-start.3
  77.5 0.1 add.44
  77.7 13.2 %collective-permute-start.1 = (bf16[4,64,128]{2,1,0:T(8,128)(2,1)S(1)}, bf16[4,64,128]{2,1,0:T(8,128)(2,1)S(1)}, u32[]{:S(2)}, u32[]{:S(2)}) collective-permute-start(bf16[4,64,128]{2,1,0:T(8,128)(2,1)S(1)} %get-tuple-element.16), channel_id=1, source_target_pairs={{0,256},{128,384},{256,0},{384,128},{1,257},{129,385},{257,1},{385... | collective-permute-start | bytes 196616 | tf_op jit(solution)/shard_map/ppermute | solution.py:275
  90.8 4.3 %collective-permute-start.2 = (bf16[4,64,128]{2,1,0:T(8,128)(2,1)S(1)}, bf16[4,64,128]{2,1,0:T(8,128)(2,1)S(1)}, u32[]{:S(2)}, u32[]{:S(2)}) collective-permute-start(bf16[4,64,128]{2,1,0:T(8,128)(2,1)S(1)} %get-tuple-element.18), channel_id=1, source_target_pairs={{0,128},{128,256},{256,384},{384,0},{1,129},{129,257},{257,385},{3... | collective-permute-start | bytes 196616 | tf_op jit(solution)/shard_map/ppermute | solution.py:275
  95.1 5.5 %collective-permute-start.3 = (bf16[4,64,128]{2,1,0:T(8,128)(2,1)S(1)}, bf16[4,64,128]{2,1,0:T(8,128)(2,1)S(1)}, u32[]{:S(2)}, u32[]{:S(2)}) collective-permute-start(bf16[4,64,128]{2,1,0:T(8,128)(2,1)S(1)} %get-tuple-element.17), channel_id=1, source_target_pairs={{0,384},{128,0},{256,128},{384,256},{1,385},{129,1},{257,129},{385... | collective-permute-start | bytes 196616 | tf_op jit(solution)/shard_map/ppermute | solution.py:275
  100.6 0.0 copy-done.2
  100.6 0.0 copy-done.3
  100.6 0.0 copy-start.1
  100.6 0.9 multiply_convert_fusion
  101.5 0.0 copy-start
  101.6 0.0 collective-permute-done.1
  101.6 0.1 collective-permute-done.2
  101.6 7.7 %collective-permute-done.3 = bf16[4,64,128]{2,1,0:T(8,128)(2,1)S(1)} collective-permute-done((bf16[4,64,128]{2,1,0:T(8,128)(2,1)S(1)}, bf16[4,64,128]{2,1,0:T(8,128)(2,1)S(1)}, u32[]{:S(2)}, u32[]{:S(2)}) %collective-permute-start.3) | collective-permute-done | bytes 65568 | tf_op jit(solution)/shard_map/ppermute | solution.py:275
  109.4 0.7 copy.13
  110.1 0.0 all-to-all-done.1.back_ref
  110.1 0.0 copy-done.1
  110.1 0.0 copy-done
  110.1 1.8 %post.1 = (bf16[128,2048]{1,0:T(8,128)(2,1)}, bf16[128,2048]{1,0:T(8,128)(2,1)}) custom-call(bf16[64,32,128]{2,1,0:T(8,128)(2,1)S(1)} %all-to-all-done.1.back_ref, bf16[128,2048]{1,0:T(8,128)(2,1)S(1)} %bitcast.27, bf16[128,2048]{1,0:T(8,128)(2,1)S(1)} %bitcast.29), custom_call_target="tpu_custom_call" | custom-call | bytes 2621440 | tf_op jit(solution)/shard_map/post/pallas_call | solution.py:55
  (2 shorter events, 0.1 us)
Async XLA Ops:
  4.1 27.4 %all-to-all-start = ((bf16[64,32,128]{2,1,0:T(8,128)(2,1)}), bf16[64,32,128]{2,1,0:T(8,128)(2,1)S(1)}, u32[]{:S(2)}, u32[]{:S(2)}) async-start(bf16[64,32,128]{2,1,0:T(8,128)(2,1)} %shard_map.93), calls=%async_computation | async-start | bytes 1048576 | tf_op jit(solution)/shard_map/all_to_all | solution.py:284
  19.4 19.4 %copy-start.4 = (bf16[32,8192]{1,0:T(8,128)(2,1)S(1)}, bf16[32,8192]{1,0:T(8,128)(2,1)}, u32[]{:S(2)}) copy-start(bf16[32,8192]{1,0:T(8,128)(2,1)} %param.11) | copy-start | bytes 1572868
  31.5 22.2 %all-to-all-start.2 = ((bf16[64,32,128]{2,1,0:T(8,128)(2,1)}), bf16[64,32,128]{2,1,0:T(8,128)(2,1)S(1)}, u32[]{:S(2)}, u32[]{:S(2)}) async-start(bf16[64,32,128]{2,1,0:T(8,128)(2,1)} %shard_map.94), calls=%async_computation.2 | async-start | bytes 1048576 | tf_op jit(solution)/shard_map/all_to_all | solution.py:288
  53.7 56.4 %all-to-all-start.1 = ((bf16[64,32,128]{2,1,0:T(8,128)(2,1)}), bf16[64,32,128]{2,1,0:T(8,128)(2,1)S(1)}, u32[]{:S(2)}, u32[]{:S(2)}) async-start(bf16[64,32,128]{2,1,0:T(8,128)(2,1)} %get-tuple-element.10), calls=%async_computation.1 | async-start | bytes 1048576 | tf_op jit(solution)/shard_map/all_to_all | solution.py:292
  69.3 8.2 %collective-permute-start = (f32[16,64,128]{2,1,0:T(8,128)S(1)}, f32[16,64,128]{2,1,0:T(8,128)S(1)}, u32[]{:S(2)}, u32[]{:S(2)}) collective-permute-start(f32[16,64,128]{2,1,0:T(8,128)S(1)} %get-tuple-element.15), channel_id=1, source_target_pairs={{0,64},{64,0},{1,65},{65,1},{2,66},{66,2},{3,67},{67,3},{4,68},{68... | collective-permute-start | bytes 1572872 | tf_op jit(solution)/shard_map/ppermute | solution.py:296
  77.5 23.1 %copy-start.2 = (bf16[1,128,2048]{2,1,0:T(8,128)(2,1)S(1)}, bf16[1,128,2048]{2,1,0:T(8,128)(2,1)}, u32[]{:S(2)}) copy-start(bf16[1,128,2048]{2,1,0:T(8,128)(2,1)} %param.10) | copy-start | bytes 1572868
  77.5 23.1 %copy-start.3 = (bf16[1,128,2048]{2,1,0:T(8,128)(2,1)S(1)}, bf16[1,128,2048]{2,1,0:T(8,128)(2,1)}, u32[]{:S(2)}) copy-start(bf16[1,128,2048]{2,1,0:T(8,128)(2,1)} %param.9) | copy-start | bytes 1572868
  77.7 23.9 %collective-permute-start.1 = (bf16[4,64,128]{2,1,0:T(8,128)(2,1)S(1)}, bf16[4,64,128]{2,1,0:T(8,128)(2,1)S(1)}, u32[]{:S(2)}, u32[]{:S(2)}) collective-permute-start(bf16[4,64,128]{2,1,0:T(8,128)(2,1)S(1)} %get-tuple-element.16), channel_id=1, source_target_pairs={{0,256},{128,384},{256,0},{384,128},{1,257},{129,385},{257,1},{385... | collective-permute-start | bytes 196616 | tf_op jit(solution)/shard_map/ppermute | solution.py:275
  90.8 10.8 %collective-permute-start.2 = (bf16[4,64,128]{2,1,0:T(8,128)(2,1)S(1)}, bf16[4,64,128]{2,1,0:T(8,128)(2,1)S(1)}, u32[]{:S(2)}, u32[]{:S(2)}) collective-permute-start(bf16[4,64,128]{2,1,0:T(8,128)(2,1)S(1)} %get-tuple-element.18), channel_id=1, source_target_pairs={{0,128},{128,256},{256,384},{384,0},{1,129},{129,257},{257,385},{3... | collective-permute-start | bytes 196616 | tf_op jit(solution)/shard_map/ppermute | solution.py:275
  95.1 14.2 %collective-permute-start.3 = (bf16[4,64,128]{2,1,0:T(8,128)(2,1)S(1)}, bf16[4,64,128]{2,1,0:T(8,128)(2,1)S(1)}, u32[]{:S(2)}, u32[]{:S(2)}) collective-permute-start(bf16[4,64,128]{2,1,0:T(8,128)(2,1)S(1)} %get-tuple-element.17), channel_id=1, source_target_pairs={{0,384},{128,0},{256,128},{384,256},{1,385},{129,1},{257,129},{385... | collective-permute-start | bytes 196616 | tf_op jit(solution)/shard_map/ppermute | solution.py:275
  100.6 9.5 %copy-start.1 = (bf16[1,128,2048]{2,1,0:T(8,128)(2,1)S(1)}, bf16[1,128,2048]{2,1,0:T(8,128)(2,1)}, u32[]{:S(2)}) copy-start(bf16[1,128,2048]{2,1,0:T(8,128)(2,1)} %param.8) | copy-start | bytes 1572868
  101.5 8.6 %copy-start = (bf16[1,128,2048]{2,1,0:T(8,128)(2,1)S(1)}, bf16[1,128,2048]{2,1,0:T(8,128)(2,1)}, u32[]{:S(2)}) copy-start(bf16[1,128,2048]{2,1,0:T(8,128)(2,1)} %param.6) | copy-start | bytes 1572868

commit v2 on v1

v2 whole, which is shorter than its diff:
```python
import functools

import jax
import jax.numpy as jnp
from jax import lax
from jax.experimental import pallas as pl
from jax.experimental.pallas import tpu as pltpu
from jax.sharding import Mesh
from jax.sharding import PartitionSpec as P


L = 128
R = 64
CH = 32
DP = ("zh", "core")
CTX = ("zl", "y", "x")
F32 = jnp.float32
BF16 = jnp.bfloat16
VMEM_LIMIT = 16 << 20
GROUPS = ((0, 1), (2, 3))


def pre_body(gate_ref, value_ref, grad_ref, post_ref, send_ref):
    width = gate_ref.shape[1]
    mixed = (gate_ref[...].astype(F32) * value_ref[...].astype(F32)).astype(BF16).T
    grad = (grad_ref[...].astype(F32) * post_ref[...].astype(F32)).astype(BF16).T
    send_ref[:, :CH, :] = mixed.reshape(width // CH, CH, L)
    send_ref[:, CH:, :] = grad.reshape(width // CH, CH, L)


def pre(gate, value, grad, post):
    channels = gate.shape[1]
    width = 1024
    block = pl.BlockSpec((L, width), lambda i: (0, i))
    return pl.pallas_call(
        pre_body,
        grid=(channels // width,),
        in_specs=[block] * 4,
        out_specs=pl.BlockSpec((width // CH, 2 * CH, L), lambda i: (i, 0, 0)),
        out_shape=jax.ShapeDtypeStruct((channels // CH, 2 * CH, L), BF16),
        cost_estimate=pl.CostEstimate(flops=0, bytes_accessed=6 * channels * L * 2, transcendentals=0),
        name="pre",
    )(gate, value, grad, post)


def post_body(back_ref, gate_ref, value_ref, d_pre_ref, d_val_ref):
    width = gate_ref.shape[1]
    back = back_ref[...].reshape(width, L).T.astype(F32)
    d_pre_ref[...] = (back * value_ref[...].astype(F32)).astype(BF16)
    d_val_ref[...] = (back * gate_ref[...].astype(F32)).astype(BF16)


def post(back, gate, value):
    channels = gate.shape[1]
    width = 1024
    block = pl.BlockSpec((L, width), lambda i: (0, i))
    shape = jax.ShapeDtypeStruct((L, channels), BF16)
    return pl.pallas_call(
        post_body,
        grid=(channels // width,),
        in_specs=[pl.BlockSpec((width // CH, CH, L), lambda i: (i, 0, 0)), block, block],
        out_specs=(block, block),
        out_shape=(shape, shape),
        cost_estimate=pl.CostEstimate(flops=0, bytes_accessed=5 * channels * L * 2, transcendentals=0),
        compiler_params=pltpu.CompilerParams(vmem_limit_bytes=VMEM_LIMIT),
        name="post",
    )(back, gate, value)


def channel_of(n, core):
    return lax.div(n, 4) * 8 + core * 4 + lax.rem(n, 4)


def shifts(rows_ref, out):
    lane = lax.broadcasted_iota(jnp.int32, (8, L), 1)
    sub = lax.broadcasted_iota(jnp.int32, (8, L), 0)
    for j in range(R):
        h, i = divmod(j, 8)
        here = rows_ref[pl.ds(8 + j, 8, stride=0), :]
        before = rows_ref[pl.ds(7 + j, 8, stride=0), :]
        shifted = [
            pltpu.roll(jnp.where(lane < L - 8 * p - sub, here, before), 8 * p, 1, stride=1, stride_axis=0)
            for p in range(2)
        ]
        out[h, pl.ds(16 * i, 16), :] = jnp.concatenate(shifted, axis=0).astype(BF16)


def taps_body(core_ref, taps_ref, other_ref, own_ref, *rows):
    core = core_ref[0]
    for r in rows:
        r[pl.ds(0, 8), :] = jnp.zeros((8, L), F32)

    def step(n, _):
        for r, out, side in ((rows[0], other_ref, 1 - core), (rows[1], own_ref, core)):
            r[pl.ds(8, R), :] = taps_ref[channel_of(n, side)].astype(F32)
            shifts(r, out.at[n])
        return 0

    lax.fori_loop(0, CH // 2, step, 0)


def shift_taps(core, taps):
    shape = jax.ShapeDtypeStruct((CH // 2, 8, L, L), BF16)
    return pl.pallas_call(
        taps_body,
        in_specs=[SCALAR, WHOLE],
        out_specs=(WHOLE, WHOLE),
        out_shape=(shape, shape),
        scratch_shapes=[pltpu.VMEM((R + 8, L), F32)] * 2,
        cost_estimate=pl.CostEstimate(flops=0, bytes_accessed=8 << 20, transcendentals=0),
        compiler_params=pltpu.CompilerParams(vmem_limit_bytes=VMEM_LIMIT),
        name="shift_taps",
    )(core, taps)


def correlate(count, load_grad, load_mixed, taps_ref, store, halves):
    lane8 = lax.broadcasted_iota(jnp.int32, (8, L), 1)
    sub8 = lax.broadcasted_iota(jnp.int32, (8, L), 0)
    lane = lax.broadcasted_iota(jnp.int32, (R, L), 1)
    for gp, vp, w, rhs, acc in halves:
        gp[pl.ds(R, 8), :] = jnp.zeros((8, L), F32)
        vp[pl.ds(0, 8), :] = jnp.zeros((8, L), F32)
        w[:, pl.ds(4, 1)] = jnp.zeros((2, 1, L, L), BF16)

    def build(n, half):
        gp, vp, w, rhs, _ = halves[half]
        gp[pl.ds(0, R), :] = load_grad(n)
        vp[pl.ds(8, R), :] = load_mixed(n)
        rows = gp[pl.ds(0, R), :]
        following = gp[pl.ds(1, R), :]
        for u in range(8):
            x = rows
            if u:
                x = pltpu.roll(jnp.where(lane >= 16 * u, rows, following), L - 16 * u, 1)
            even = x.astype(BF16)
            odd = jnp.concatenate([x[8:], jnp.zeros((8, L), F32)], axis=0).astype(BF16)
            for t in range(4):
                w[0, t, pl.ds(16 * u, 16), :] = even[16 * t : 16 * t + 16]
                w[1, t, pl.ds(16 * u, 16), :] = odd[16 * t : 16 * t + 16]
        shifts(vp, rhs)

    def multiply(n, half):
        _, _, w, rhs, acc = halves[half]

        def columns(h):
            pieces = [ref[h, pl.ds(16 * i, 16), :] for i in range(8) for ref in (taps_ref.at[n], rhs)]
            return jnp.concatenate(pieces, axis=0)

        for group in GROUPS:
            depth = 4 - group[0]
            lhs = jnp.concatenate(
                [
                    jnp.concatenate([w[k, min(p + h, 4)] for h in range(depth) for k in range(2)], axis=1)
                    for p in group
                ],
                axis=0,
            )
            cols = jnp.concatenate([columns(h) for h in range(2 * depth)], axis=1)
            out = lax.dot_general(lhs, cols, (((1,), (1,)), ((), ())), preferred_element_type=F32)
            for m, p in enumerate(group):
                acc[0, p] = out[L * m : L * m + L, :L]
                acc[1, p] = out[L * m : L * m + L, L:]

    def finish(n, half):
        _, _, _, _, acc = halves[half]
        tops = []
        for u in range(8):
            lo, hi = ([acc[k, p, pl.ds(16 * u, 16), :] for p in range(4)] for k in range(2))
            lo = [jnp.where(sub8 >= lane8 // 32, lo[0][:8], 0.0), lo[0][8:]] + lo[1:]
            hi = [jnp.where(sub8 >= lane8 // 32 + 4, hi[0][:8], 0.0), hi[0][8:]] + hi[1:]
            tops.append(jnp.concatenate(lo, axis=0) + pltpu.roll(jnp.concatenate(hi, axis=0), R - 4, 0))

        def pair(p, q, width):
            low = (lane & width) == 0
            a = jnp.where(low, p, q)
            b = jnp.where(low, q, p)
            right = pltpu.roll(b, width, 1)
            left = right if 2 * width == L else pltpu.roll(b, L - width, 1)
            return jnp.where(low, a, right) + pltpu.roll(jnp.where(low, left, a), R - width // 32, 0)

        even = pair(pair(tops[0], tops[4], 64), pair(tops[2], tops[6], 64), 32)
        odd = pair(pair(tops[1], tops[5], 64), pair(tops[3], tops[7], 64), 32)
        low = (lane & 16) == 0
        store(n, jnp.where(low, even, pltpu.roll(odd, 16, 1)), jnp.where(low, pltpu.roll(even, L - 16, 1), odd))

    build(0, 0)

    def step(m, _):
        n = 2 * m
        multiply(n, 0)
        build(n + 1, 1)
        finish(jnp.maximum(n - 1, 0), 1)
        multiply(n + 1, 1)
        build(jnp.minimum(n + 2, count - 1), 0)
        finish(n, 0)
        return 0

    lax.fori_loop(0, count // 2, step, 0)
    finish(count - 1, 1)


HALF = [
    pltpu.VMEM((R + 8, L), F32),
    pltpu.VMEM((R + 8, L), F32),
    pltpu.VMEM((2, 5, L, L), BF16),
    pltpu.VMEM((8, L, L), BF16),
    pltpu.VMEM((2, 4, L, L), F32),
]
WHOLE = pl.BlockSpec(memory_space=pltpu.VMEM)
SCALAR = pl.BlockSpec(memory_space=pltpu.SMEM)
CONV_COST = pl.CostEstimate(flops=CH * 256 * 1024 * 256, bytes_accessed=2 << 20, transcendentals=0)
TERMS = jax.ShapeDtypeStruct((CH // 2, R, L), F32)


def other_body(core_ref, recv_ref, taps_ref, term_ref, back_ref, rows_ref, wide, *bufs, scale, batch):
    def widen(r, _):
        at = pl.multiple_of(r * 8, 8)
        for c in range(0, 2 * CH, 16):
            x = recv_ref[pl.ds(at, 8), c : c + 16, :].astype(F32)
            wide[c : c + 16, pl.ds(at, 8), :] = jnp.swapaxes(x, 0, 1)
        return 0

    lax.fori_loop(0, R // 8, widen, 0)

    def keep(c, _):
        rows_ref[c] = wide[c].astype(BF16)
        return 0

    lax.fori_loop(0, 2 * CH, keep, 0, unroll=4)
    side = 1 - core_ref[0]

    def store(n, back, term):
        back_ref[n] = (back * scale).astype(BF16)
        term_ref[n] = term * (scale / batch)

    correlate(
        CH // 2,
        lambda n: wide[CH + channel_of(n, side)],
        lambda n: wide[channel_of(n, side)],
        taps_ref,
        store,
        (bufs[:5], bufs[5:]),
    )


def conv_other(core, recv, taps, scale, batch):
    return pl.pallas_call(
        functools.partial(other_body, scale=scale, batch=batch),
        in_specs=[SCALAR, WHOLE, WHOLE],
        out_specs=(WHOLE,) * 3,
        out_shape=(
            TERMS,
            jax.ShapeDtypeStruct((CH // 2, R, L), BF16),
            jax.ShapeDtypeStruct((2 * CH, R, L), BF16),
        ),
        scratch_shapes=[pltpu.VMEM((2 * CH, R, L), F32)] + HALF * 2,
        cost_estimate=CONV_COST,
        compiler_params=pltpu.CompilerParams(vmem_limit_bytes=VMEM_LIMIT),
        name="conv_other",
    )(core, recv, taps)


def own_body(core_ref, rows_ref, other_ref, taps_ref, term_ref, send_ref, flat, *bufs, scale, batch):
    core = core_ref[0]

    def store(n, back, term):
        flat[channel_of(n, core)] = back * scale
        term_ref[n] = term * (scale / batch)

    correlate(
        CH // 2,
        lambda n: rows_ref[CH + channel_of(n, core)].astype(F32),
        lambda n: rows_ref[channel_of(n, core)].astype(F32),
        taps_ref,
        store,
        (bufs[:5], bufs[5:]),
    )

    def fetch(n, _):
        flat[channel_of(n, 1 - core)] = other_ref[n].astype(F32)
        return 0

    lax.fori_loop(0, CH // 2, fetch, 0, unroll=2)

    def narrow(r, _):
        at = pl.multiple_of(r * 8, 8)
        for c in range(0, CH, 16):
            x = jnp.swapaxes(flat[c : c + 16, pl.ds(at, 8), :], 0, 1)
            send_ref[pl.ds(at, 8), c : c + 16, :] = x.astype(BF16)
        return 0

    lax.fori_loop(0, R // 8, narrow, 0)


def conv_own(core, rows, other, taps, scale, batch):
    return pl.pallas_call(
        functools.partial(own_body, scale=scale, batch=batch),
        in_specs=[SCALAR, WHOLE, WHOLE, WHOLE],
        out_specs=(WHOLE,) * 2,
        out_shape=(TERMS, jax.ShapeDtypeStruct((R, CH, L), BF16)),
        scratch_shapes=[pltpu.VMEM((CH, R, L), F32)] + HALF * 2,
        cost_estimate=CONV_COST,
        compiler_params=pltpu.CompilerParams(vmem_limit_bytes=VMEM_LIMIT),
        name="conv_own",
    )(core, rows, other, taps)


def last_sum_body(own_ref, far_ref, up_ref, down_ref, out_ref):
    total = own_ref[...] + (far_ref[...].astype(F32) + (up_ref[...].astype(F32) + down_ref[...].astype(F32)))
    for r in range(R):
        out_ref[:, pl.ds(L * r, L)] = total[:, r, :]


def last_sum(own, parts):
    return pl.pallas_call(
        last_sum_body,
        in_specs=[WHOLE] * 4,
        out_specs=WHOLE,
        out_shape=jax.ShapeDtypeStruct((own.shape[0], R * L), F32),
        compiler_params=pltpu.CompilerParams(vmem_limit_bytes=VMEM_LIMIT),
        name="last_sum",
    )(own, *parts)


def sum_over_zh(both):
    zh = lax.axis_index("zh")
    count = lax.axis_size("zh")
    pick = functools.partial(lax.dynamic_index_in_dim, axis=0, keepdims=False)
    parts = []
    for shift in (2, 1, 3):
        ahead = [(i, (i + shift) % count) for i in range(count)]
        parts.append(lax.ppermute(pick(both, (zh + shift) % count).astype(BF16), "zh", ahead))
    return last_sum(pick(both, zh), parts)


def local(pre_gate, post_gate, values, conv_out, grad_out, filter_param):
    gate, value, grad = pre_gate[0], values[0], grad_out[0]
    length = filter_param.shape[1]
    exchange = functools.partial(lax.all_to_all, axis_name=CTX, split_axis=0, concat_axis=0, tiled=True)
    scale = length ** (-0.5)
    batch = lax.axis_size("zh") * lax.axis_size("core")
    core = lax.axis_index("core").astype(jnp.int32).reshape(1)
    send = pre(gate, value, grad, post_gate[0])
    recv = exchange(send)
    d_post = (grad.astype(F32) * conv_out[0].astype(F32)).astype(BF16)
    taps_other, taps_own = shift_taps(core, filter_param.reshape(CH, R, L))
    terms, back, rows = conv_other(core, recv, taps_other, scale, batch)
    terms = lax.ppermute(terms, "core", [(0, 1), (1, 0)])
    own, back = conv_own(core, rows, back, taps_own, scale, batch)
    back = exchange(back)
    both = own + terms
    d_filter = sum_over_zh(both.reshape(4, 4, R, L))
    d_pre, d_val = post(back, gate, value)
    return (d_pre[None], d_post[None], d_val[None], d_filter)


def solution(mesh):
    fine = Mesh(mesh.devices.reshape(4, 2, 4, 4, 4), DP + CTX)
    tokens = P(DP, CTX, None)
    return jax.shard_map(
        local,
        mesh=fine,
        in_specs=(tokens,) * 5 + (P(CTX, None),),
        out_specs=(tokens, tokens, tokens, P(CTX + DP, None)),
        check_vma=False,
    )
```

time: 113 us -> 106 us (0.938)
  Pallas kernels: 34.6 us -> 23.3 us
  starting transfers between devices: 52.9 us -> 44 us
  waiting for transfers between devices: 21.7 us -> 27.5 us
  local copies, waits for them, and re-layouts: 0.92 us -> 6.45 us
  other arithmetic: 1.03 us -> 3.06 us
    pallas_call x5, Pallas kernels: 32.8 us -> 22 us  [the longest x1 7.87 us: conv_own(): pl.pallas_call(functools.partial(own_body, scale=scale, batch=batch), in_...]
    all_to_all x2 -> x1, starting transfers between devices: 19.1 us -> 11.8 us  [local(): recv = exchange(send)]
    unnamed x12 -> x17, local copies, waits for them, and re-layouts: 0.88 us -> 6.39 us
    all_to_all x2 -> x1, waiting for transfers between devices: 13.9 us -> 18.8 us  [local(): recv = exchange(send)]
    all_to_all x1, starting transfers between devices: 9.03 us -> 7.48 us  [local(): back = exchange(back)]
  transfers between devices with their start and end apart: 7 -> 6, of which waited for: 4 -> 3; matrix products, arithmetic and copies ran while one was open for 2% -> 3% of each run, Pallas kernels for 26% -> 4%
where the time goes in v2:
time: 106 us; the launch traced here: 105 us
  starting transfers between devices  44 us (42%)
  waiting for transfers between devices  27.5 us (26%)
  Pallas kernels  23.3 us (22%)
  local copies, waits for them, and re-layouts  6.45 us (6%)
  other arithmetic  3.06 us (3%)
    ppermute x3, starting transfers between devices, sum_over_zh(): lax.ppermute(pick(both, (zh + shift) % count).astype(BF16), 'zh', ahead)  22.8 us
    all_to_all x1, waiting for transfers between devices, local(): recv = exchange(send)  18.8 us
    all_to_all x1, starting transfers between devices, local(): recv = exchange(send)  11.8 us
    ppermute x3, waiting for transfers between devices, sum_over_zh(): lax.ppermute(pick(both, (zh + shift) % count).astype(BF16), 'zh', ahead)  8.71 us
    pallas_call x1, Pallas kernels, conv_own(): pl.pallas_call(functools.partial(own_body, scale=scale, batch=batch), in_...  7.87 us
    all_to_all x1, starting transfers between devices, local(): back = exchange(back)  7.48 us
    pallas_call x1, Pallas kernels, conv_other(): pl.pallas_call(functools.partial(other_body, scale=scale, batch=batch), i...  7.38 us
    unnamed x17, local copies, waits for them, and re-layouts  6.39 us
  transfers between devices with their start and end apart: 6, of which 3 were waited for; matrix products, arithmetic and copies ran while one was open for 3% of the time, Pallas kernels for 4%

profile of v2, /device:TPU:24, one launch (start us, length us, event | category | flops | bytes accessed | tf_op | source)
XLA Modules:
  0.0 105.1 jit_solution(9701036681015745684)
XLA Ops:
  0.6 0.0 copy-start.7
  0.6 2.6 %pre.1 = bf16[64,64,128]{2,1,0:T(8,128)(2,1)} custom-call(bf16[128,2048]{1,0:T(8,128)(2,1)} %bitcast.18, bf16[128,2048]{1,0:T(8,128)(2,1)} %bitcast.20, bf16[128,2048]{1,0:T(8,128)(2,1)} %bitcast.23, bf16[128,2048]{1,0:T(8,128)(2,1)} %bitcast.27), custom_call_target="tpu_custom_call" | custom-call | bytes 3145728 | tf_op jit(solution)/shard_map/pre/pallas_call | solution.py:35
  3.2 11.8 %all-to-all-start = ((bf16[64,64,128]{2,1,0:T(8,128)(2,1)}), bf16[64,64,128]{2,1,0:T(8,128)(2,1)S(1)}, u32[]{:S(2)}, u32[]{:S(2)}) async-start(bf16[64,64,128]{2,1,0:T(8,128)(2,1)} %pre.1), calls=%async_computation | async-start | bytes 2097152 | tf_op jit(solution)/shard_map/all_to_all | solution.py:344
  15.0 0.0 copy-done.7
  15.0 0.1 copy.10
  15.2 3.5 %shift_taps.1 = (bf16[16,8,128,128]{3,2,1,0:T(8,128)(2,1)S(1)}, bf16[16,8,128,128]{3,2,1,0:T(8,128)(2,1)S(1)}) custom-call(s32[1]{0:T(128)} %bitcast.core_ref, bf16[32,64,128]{2,1,0:T(8,128)(2,1)S(1)} %bitcast.22), custom_call_target="tpu_custom_call" | custom-call | bytes 8388608 | tf_op jit(solution)/shard_map/shift_taps/pallas_call | solution.py:104
  18.6 0.0 copy-start.2
  18.6 1.9 %copy-done.2 = bf16[16,8,128,128]{3,2,1,0:T(8,128)(2,1)} copy-done((bf16[16,8,128,128]{3,2,1,0:T(8,128)(2,1)}, bf16[16,8,128,128]{3,2,1,0:T(8,128)(2,1)S(1)}, u32[]{:S(2)}) %copy-start.2) | copy-done | bytes 4194328
  20.6 0.0 copy-start.4
  20.6 2.0 %copy-done.4 = bf16[16,8,128,128]{3,2,1,0:T(8,128)(2,1)} copy-done((bf16[16,8,128,128]{3,2,1,0:T(8,128)(2,1)}, bf16[16,8,128,128]{3,2,1,0:T(8,128)(2,1)S(1)}, u32[]{:S(2)}) %copy-start.4) | copy-done | bytes 4194328
  22.5 18.8 %all-to-all-done.recv_ref = bf16[64,64,128]{2,1,0:T(8,128)(2,1)S(1)} async-done(((bf16[64,64,128]{2,1,0:T(8,128)(2,1)}), bf16[64,64,128]{2,1,0:T(8,128)(2,1)S(1)}, u32[]{:S(2)}, u32[]{:S(2)}) %all-to-all-start) | async-done | bytes 1048608 | tf_op jit(solution)/shard_map/all_to_all | solution.py:344
  41.4 0.0 copy-start.3
  41.4 0.0 copy-start.5
  41.4 2.3 %copy-done.5 = bf16[16,8,128,128]{3,2,1,0:T(8,128)(2,1)S(1)} copy-done((bf16[16,8,128,128]{3,2,1,0:T(8,128)(2,1)S(1)}, bf16[16,8,128,128]{3,2,1,0:T(8,128)(2,1)}, u32[]{:S(2)}) %copy-start.5) | copy-done | bytes 4194328
  43.7 7.4 %conv_other.1 = (f32[16,64,128]{2,1,0:T(8,128)S(1)}, bf16[16,64,128]{2,1,0:T(8,128)(2,1)S(1)}, bf16[64,64,128]{2,1,0:T(8,128)(2,1)S(1)}) custom-call(s32[1]{0:T(128)} %bitcast.core_ref, bf16[64,64,128]{2,1,0:T(8,128)(2,1)S(1)} %all-to-all-done.recv_ref, bf16[16,8,128,128]{3,2,1,0:T(8,128)(2,1)S(1)} %copy-done.5), custom_call_target="tpu_custom_call" | custom-call | flops 2147483648 | bytes 2097152 | tf_op jit(solution)/shard_map/conv_other/pallas_call | solution.py:247
  51.1 0.0 copy-done.3
  51.1 0.0 copy-start.6
  51.1 7.9 %conv_own.1 = (f32[16,64,128]{2,1,0:T(8,128)S(1)}, bf16[64,32,128]{2,1,0:T(8,128)(2,1)}) custom-call(s32[1]{0:T(128)} %bitcast.core_ref, bf16[64,64,128]{2,1,0:T(8,128)(2,1)S(1)} %get-tuple-element.14.rows_ref, bf16[16,64,128]{2,1,0:T(8,128)(2,1)S(1)} %get-tuple-element.15.other_ref, bf16[16,8,128,128]{3,2,1,0:T(8,128)(2,1)S(1)} %copy-done.3), custom_call_target="tpu_custom_call" | custom-call | flops 2147483648 | bytes 2097152 | tf_op jit(solution)/shard_map/conv_own/pallas_call | solution.py:296
  59.0 0.0 copy-start
  59.0 0.0 copy-start.1
  59.0 7.5 %all-to-all-start.1 = ((bf16[64,32,128]{2,1,0:T(8,128)(2,1)}), bf16[64,32,128]{2,1,0:T(8,128)(2,1)S(1)}, u32[]{:S(2)}, u32[]{:S(2)}) async-start(bf16[64,32,128]{2,1,0:T(8,128)(2,1)} %get-tuple-element.17), calls=%async_computation.1 | async-start | bytes 1048576 | tf_op jit(solution)/shard_map/all_to_all | solution.py:350
  66.5 1.9 %collective-permute-start = (f32[16,64,128]{2,1,0:T(8,128)S(1)}, f32[16,64,128]{2,1,0:T(8,128)}, u32[]{:S(2)}, u32[]{:S(2)}) collective-permute-start(f32[16,64,128]{2,1,0:T(8,128)S(1)} %get-tuple-element.21), channel_id=1, source_target_pairs={{0,64},{64,0},{1,65},{65,1},{2,66},{66,2},{3,67},{67,3},{4,68},{68... | collective-permute-start | bytes 1572872 | tf_op jit(solution)/shard_map/ppermute | solution.py:348
  68.4 0.0 copy-done.6
  68.5 2.0 %multiply_convert_fusion = bf16[1,128,2048]{2,1,0:T(8,128)(2,1)} fusion(bf16[1,128,2048]{2,1,0:T(8,128)(2,1)} %param.9, bf16[1,128,2048]{2,1,0:T(8,128)(2,1)S(1)} %copy-done.6), kind=kLoop, calls=%fused_computation | loop fusion | flops 1048576 | bytes 1572864 | tf_op jit(solution)/shard_map/convert_element_type | solution.py:345
  70.4 0.0 collective-permute-done
  70.4 1.1 %add.35 = f32[16,64,128]{2,1,0:T(8,128)S(1)} add(f32[16,64,128]{2,1,0:T(8,128)S(1)} %get-tuple-element.20, f32[16,64,128]{2,1,0:T(8,128)} %collective-permute-done) | non-fusion elementwise | flops 131072 | bytes 1572864 | tf_op jit(solution)/shard_map/add | solution.py:351
  71.6 13.0 %collective-permute-start.1 = (bf16[4,64,128]{2,1,0:T(8,128)(2,1)S(1)}, bf16[4,64,128]{2,1,0:T(8,128)(2,1)S(1)}, u32[]{:S(2)}, u32[]{:S(2)}) collective-permute-start(bf16[4,64,128]{2,1,0:T(8,128)(2,1)S(1)} %get-tuple-element.24), channel_id=1, source_target_pairs={{0,256},{128,384},{256,0},{384,128},{1,257},{129,385},{257,1},{385... | collective-permute-start | bytes 196616 | tf_op jit(solution)/shard_map/ppermute | solution.py:332
  84.6 4.3 %collective-permute-start.2 = (bf16[4,64,128]{2,1,0:T(8,128)(2,1)S(1)}, bf16[4,64,128]{2,1,0:T(8,128)(2,1)S(1)}, u32[]{:S(2)}, u32[]{:S(2)}) collective-permute-start(bf16[4,64,128]{2,1,0:T(8,128)(2,1)S(1)} %get-tuple-element.23), channel_id=1, source_target_pairs={{0,128},{128,256},{256,384},{384,0},{1,129},{129,257},{257,385},{3... | collective-permute-start | bytes 196616 | tf_op jit(solution)/shard_map/ppermute | solution.py:332
  88.9 5.5 %collective-permute-start.3 = (bf16[4,64,128]{2,1,0:T(8,128)(2,1)S(1)}, bf16[4,64,128]{2,1,0:T(8,128)(2,1)S(1)}, u32[]{:S(2)}, u32[]{:S(2)}) collective-permute-start(bf16[4,64,128]{2,1,0:T(8,128)(2,1)S(1)} %get-tuple-element.22), channel_id=1, source_target_pairs={{0,384},{128,0},{256,128},{384,256},{1,385},{129,1},{257,129},{385... | collective-permute-start | bytes 196616 | tf_op jit(solution)/shard_map/ppermute | solution.py:332
  94.4 0.0 collective-permute-done.1.far_ref
  94.4 1.0 collective-permute-done.2.up_ref
  95.4 7.7 %collective-permute-done.3.down_ref = bf16[4,64,128]{2,1,0:T(8,128)(2,1)S(1)} collective-permute-done((bf16[4,64,128]{2,1,0:T(8,128)(2,1)S(1)}, bf16[4,64,128]{2,1,0:T(8,128)(2,1)S(1)}, u32[]{:S(2)}, u32[]{:S(2)}) %collective-permute-start.3) | collective-permute-done | bytes 65568 | tf_op jit(solution)/shard_map/ppermute | solution.py:332
  103.1 0.7 last_sum.1
  103.9 0.0 all-to-all-done.1.back_ref
  103.9 0.0 copy-done
  103.9 0.0 copy-done.1
  103.9 1.2 %post.1 = (bf16[128,2048]{1,0:T(8,128)(2,1)}, bf16[128,2048]{1,0:T(8,128)(2,1)}) custom-call(bf16[64,32,128]{2,1,0:T(8,128)(2,1)S(1)} %all-to-all-done.1.back_ref, bf16[128,2048]{1,0:T(8,128)(2,1)S(1)} %bitcast.19, bf16[128,2048]{1,0:T(8,128)(2,1)S(1)} %bitcast.21), custom_call_target="tpu_custom_call" | custom-call | bytes 2621440 | tf_op jit(solution)/shard_map/post/pallas_call | solution.py:58
  (2 shorter events, 0.1 us)
Async XLA Ops:
  0.6 14.4 %copy-start.7 = (bf16[32,8192]{1,0:T(8,128)(2,1)S(1)}, bf16[32,8192]{1,0:T(8,128)(2,1)}, u32[]{:S(2)}) copy-start(bf16[32,8192]{1,0:T(8,128)(2,1)} %param.11) | copy-start | bytes 1572868
  3.2 38.1 %all-to-all-start = ((bf16[64,64,128]{2,1,0:T(8,128)(2,1)}), bf16[64,64,128]{2,1,0:T(8,128)(2,1)S(1)}, u32[]{:S(2)}, u32[]{:S(2)}) async-start(bf16[64,64,128]{2,1,0:T(8,128)(2,1)} %pre.1), calls=%async_computation | async-start | bytes 2097152 | tf_op jit(solution)/shard_map/all_to_all | solution.py:344
  18.6 1.9 %copy-start.2 = (bf16[16,8,128,128]{3,2,1,0:T(8,128)(2,1)}, bf16[16,8,128,128]{3,2,1,0:T(8,128)(2,1)S(1)}, u32[]{:S(2)}) copy-start(bf16[16,8,128,128]{3,2,1,0:T(8,128)(2,1)S(1)} %get-tuple-element.16.taps_ref) | copy-start | bytes 12582916
  20.6 2.0 %copy-start.4 = (bf16[16,8,128,128]{3,2,1,0:T(8,128)(2,1)}, bf16[16,8,128,128]{3,2,1,0:T(8,128)(2,1)S(1)}, u32[]{:S(2)}) copy-start(bf16[16,8,128,128]{3,2,1,0:T(8,128)(2,1)S(1)} %get-tuple-element.13.taps_ref) | copy-start | bytes 12582916
  41.4 9.7 %copy-start.3 = (bf16[16,8,128,128]{3,2,1,0:T(8,128)(2,1)S(1)}, bf16[16,8,128,128]{3,2,1,0:T(8,128)(2,1)}, u32[]{:S(2)}) copy-start(bf16[16,8,128,128]{3,2,1,0:T(8,128)(2,1)} %copy-done.2) | copy-start | bytes 12582916
  41.4 2.3 %copy-start.5 = (bf16[16,8,128,128]{3,2,1,0:T(8,128)(2,1)S(1)}, bf16[16,8,128,128]{3,2,1,0:T(8,128)(2,1)}, u32[]{:S(2)}) copy-start(bf16[16,8,128,128]{3,2,1,0:T(8,128)(2,1)} %copy-done.4) | copy-start | bytes 12582916
  51.1 17.4 %copy-start.6 = (bf16[1,128,2048]{2,1,0:T(8,128)(2,1)S(1)}, bf16[1,128,2048]{2,1,0:T(8,128)(2,1)}, u32[]{:S(2)}) copy-start(bf16[1,128,2048]{2,1,0:T(8,128)(2,1)} %param.10) | copy-start | bytes 1572868
  59.0 44.9 %copy-start = (bf16[1,128,2048]{2,1,0:T(8,128)(2,1)S(1)}, bf16[1,128,2048]{2,1,0:T(8,128)(2,1)}, u32[]{:S(2)}) copy-start(bf16[1,128,2048]{2,1,0:T(8,128)(2,1)} %param.6) | copy-start | bytes 1572868
  59.0 44.9 %copy-start.1 = (bf16[1,128,2048]{2,1,0:T(8,128)(2,1)S(1)}, bf16[1,128,2048]{2,1,0:T(8,128)(2,1)}, u32[]{:S(2)}) copy-start(bf16[1,128,2048]{2,1,0:T(8,128)(2,1)} %param.8) | copy-start | bytes 1572868
  59.0 44.9 %all-to-all-start.1 = ((bf16[64,32,128]{2,1,0:T(8,128)(2,1)}), bf16[64,32,128]{2,1,0:T(8,128)(2,1)S(1)}, u32[]{:S(2)}, u32[]{:S(2)}) async-start(bf16[64,32,128]{2,1,0:T(8,128)(2,1)} %get-tuple-element.17), calls=%async_computation.1 | async-start | bytes 1048576 | tf_op jit(solution)/shard_map/all_to_all | solution.py:350
  66.5 4.0 %collective-permute-start = (f32[16,64,128]{2,1,0:T(8,128)S(1)}, f32[16,64,128]{2,1,0:T(8,128)}, u32[]{:S(2)}, u32[]{:S(2)}) collective-permute-start(f32[16,64,128]{2,1,0:T(8,128)S(1)} %get-tuple-element.21), channel_id=1, source_target_pairs={{0,64},{64,0},{1,65},{65,1},{2,66},{66,2},{3,67},{67,3},{4,68},{68... | collective-permute-start | bytes 1572872 | tf_op jit(solution)/shard_map/ppermute | solution.py:348
  71.6 22.8 %collective-permute-start.1 = (bf16[4,64,128]{2,1,0:T(8,128)(2,1)S(1)}, bf16[4,64,128]{2,1,0:T(8,128)(2,1)S(1)}, u32[]{:S(2)}, u32[]{:S(2)}) collective-permute-start(bf16[4,64,128]{2,1,0:T(8,128)(2,1)S(1)} %get-tuple-element.24), channel_id=1, source_target_pairs={{0,256},{128,384},{256,0},{384,128},{1,257},{129,385},{257,1},{385... | collective-permute-start | bytes 196616 | tf_op jit(solution)/shard_map/ppermute | solution.py:332
  84.6 10.8 %collective-permute-start.2 = (bf16[4,64,128]{2,1,0:T(8,128)(2,1)S(1)}, bf16[4,64,128]{2,1,0:T(8,128)(2,1)S(1)}, u32[]{:S(2)}, u32[]{:S(2)}) collective-permute-start(bf16[4,64,128]{2,1,0:T(8,128)(2,1)S(1)} %get-tuple-element.23), channel_id=1, source_target_pairs={{0,128},{128,256},{256,384},{384,0},{1,129},{129,257},{257,385},{3... | collective-permute-start | bytes 196616 | tf_op jit(solution)/shard_map/ppermute | solution.py:332
  88.9 14.2 %collective-permute-start.3 = (bf16[4,64,128]{2,1,0:T(8,128)(2,1)S(1)}, bf16[4,64,128]{2,1,0:T(8,128)(2,1)S(1)}, u32[]{:S(2)}, u32[]{:S(2)}) collective-permute-start(bf16[4,64,128]{2,1,0:T(8,128)(2,1)S(1)} %get-tuple-element.22), channel_id=1, source_target_pairs={{0,384},{128,0},{256,128},{384,256},{1,385},{129,1},{257,129},{385... | collective-permute-start | bytes 196616 | tf_op jit(solution)/shard_map/ppermute | solution.py:332

commit v3 on v2

--- a/solution.py
+++ b/solution.py
@@ -217,16 +217,12 @@
         at = pl.multiple_of(r * 8, 8)
         for c in range(0, 2 * CH, 16):
             x = recv_ref[pl.ds(at, 8), c : c + 16, :].astype(F32)
-            wide[c : c + 16, pl.ds(at, 8), :] = jnp.swapaxes(x, 0, 1)
-        return 0
-
-    lax.fori_loop(0, R // 8, widen, 0)
-
-    def keep(c, _):
-        rows_ref[c] = wide[c].astype(BF16)
-        return 0
-
-    lax.fori_loop(0, 2 * CH, keep, 0, unroll=4)
+            x = jnp.swapaxes(x, 0, 1)
+            wide[c : c + 16, pl.ds(at, 8), :] = x
+            rows_ref[c : c + 16, pl.ds(at, 8), :] = x.astype(BF16)
+        return 0
+
+    lax.fori_loop(0, R // 8, widen, 0, unroll=2)
     side = 1 - core_ref[0]
 
     def store(n, back, term):
@@ -289,7 +285,7 @@
             send_ref[pl.ds(at, 8), c : c + 16, :] = x.astype(BF16)
         return 0
 
-    lax.fori_loop(0, R // 8, narrow, 0)
+    lax.fori_loop(0, R // 8, narrow, 0, unroll=2)
 
 
 def conv_own(core, rows, other, taps, scale, batch):

time: 106 us -> 105 us (level)
  no operation moved by 1% of the time
where the time goes in v3:
time: 105 us
  starting transfers between devices  44 us (42%)
  waiting for transfers between devices  27.5 us (26%)
  Pallas kernels  23.1 us (22%)
  local copies, waits for them, and re-layouts  6.45 us (6%)
  other arithmetic  3.06 us (3%)
    ppermute x3, starting transfers between devices, sum_over_zh(): lax.ppermute(pick(both, (zh + shift) % count).astype(BF16), 'zh', ahead)  22.8 us
    all_to_all x1, waiting for transfers between devices, local(): recv = exchange(send)  18.8 us
    all_to_all x1, starting transfers between devices, local(): recv = exchange(send)  11.8 us
    ppermute x3, waiting for transfers between devices, sum_over_zh(): lax.ppermute(pick(both, (zh + shift) % count).astype(BF16), 'zh', ahead)  8.71 us
    pallas_call x1, Pallas kernels, conv_own(): pl.pallas_call(functools.partial(own_body, scale=scale, batch=batch), in_...  7.84 us
    all_to_all x1, starting transfers between devices, local(): back = exchange(back)  7.48 us
    pallas_call x1, Pallas kernels, conv_other(): pl.pallas_call(functools.partial(other_body, scale=scale, batch=batch), i...  7.29 us
    unnamed x17, local copies, waits for them, and re-layouts  6.39 us
  transfers between devices with their start and end apart: 6, of which 3 were waited for; matrix products, arithmetic and copies ran while one was open for 3% of the time, Pallas kernels for 4%

profile of v3, /device:TPU:24, one launch (start us, length us, event | category | flops | bytes accessed | tf_op | source)
XLA Modules:
  0.0 105.0 jit_solution(11907343759436620087)
XLA Ops:
  0.6 0.0 copy-start.7
  0.6 2.6 %pre.1 = bf16[64,64,128]{2,1,0:T(8,128)(2,1)} custom-call(bf16[128,2048]{1,0:T(8,128)(2,1)} %bitcast.18, bf16[128,2048]{1,0:T(8,128)(2,1)} %bitcast.20, bf16[128,2048]{1,0:T(8,128)(2,1)} %bitcast.23, bf16[128,2048]{1,0:T(8,128)(2,1)} %bitcast.27), custom_call_target="tpu_custom_call" | custom-call | bytes 3145728 | tf_op jit(solution)/shard_map/pre/pallas_call | solution.py:35
  3.2 11.8 %all-to-all-start = ((bf16[64,64,128]{2,1,0:T(8,128)(2,1)}), bf16[64,64,128]{2,1,0:T(8,128)(2,1)S(1)}, u32[]{:S(2)}, u32[]{:S(2)}) async-start(bf16[64,64,128]{2,1,0:T(8,128)(2,1)} %pre.1), calls=%async_computation | async-start | bytes 2097152 | tf_op jit(solution)/shard_map/all_to_all | solution.py:340
  15.0 0.0 copy-done.7
  15.0 0.1 copy.10
  15.2 3.5 %shift_taps.1 = (bf16[16,8,128,128]{3,2,1,0:T(8,128)(2,1)S(1)}, bf16[16,8,128,128]{3,2,1,0:T(8,128)(2,1)S(1)}) custom-call(s32[1]{0:T(128)} %bitcast.core_ref, bf16[32,64,128]{2,1,0:T(8,128)(2,1)S(1)} %bitcast.22), custom_call_target="tpu_custom_call" | custom-call | bytes 8388608 | tf_op jit(solution)/shard_map/shift_taps/pallas_call | solution.py:104
  18.6 0.0 copy-start.2
  18.6 1.9 %copy-done.2 = bf16[16,8,128,128]{3,2,1,0:T(8,128)(2,1)} copy-done((bf16[16,8,128,128]{3,2,1,0:T(8,128)(2,1)}, bf16[16,8,128,128]{3,2,1,0:T(8,128)(2,1)S(1)}, u32[]{:S(2)}) %copy-start.2) | copy-done | bytes 4194328
  20.6 0.0 copy-start.4
  20.6 2.0 %copy-done.4 = bf16[16,8,128,128]{3,2,1,0:T(8,128)(2,1)} copy-done((bf16[16,8,128,128]{3,2,1,0:T(8,128)(2,1)}, bf16[16,8,128,128]{3,2,1,0:T(8,128)(2,1)S(1)}, u32[]{:S(2)}) %copy-start.4) | copy-done | bytes 4194328
  22.5 18.8 %all-to-all-done.recv_ref = bf16[64,64,128]{2,1,0:T(8,128)(2,1)S(1)} async-done(((bf16[64,64,128]{2,1,0:T(8,128)(2,1)}), bf16[64,64,128]{2,1,0:T(8,128)(2,1)S(1)}, u32[]{:S(2)}, u32[]{:S(2)}) %all-to-all-start) | async-done | bytes 1048608 | tf_op jit(solution)/shard_map/all_to_all | solution.py:340
  41.4 0.0 copy-start.3
  41.4 0.0 copy-start.5
  41.4 2.3 %copy-done.5 = bf16[16,8,128,128]{3,2,1,0:T(8,128)(2,1)S(1)} copy-done((bf16[16,8,128,128]{3,2,1,0:T(8,128)(2,1)S(1)}, bf16[16,8,128,128]{3,2,1,0:T(8,128)(2,1)}, u32[]{:S(2)}) %copy-start.5) | copy-done | bytes 4194328
  43.7 7.3 %conv_other.1 = (f32[16,64,128]{2,1,0:T(8,128)S(1)}, bf16[16,64,128]{2,1,0:T(8,128)(2,1)S(1)}, bf16[64,64,128]{2,1,0:T(8,128)(2,1)S(1)}) custom-call(s32[1]{0:T(128)} %bitcast.core_ref, bf16[64,64,128]{2,1,0:T(8,128)(2,1)S(1)} %all-to-all-done.recv_ref, bf16[16,8,128,128]{3,2,1,0:T(8,128)(2,1)S(1)} %copy-done.5), custom_call_target="tpu_custom_call" | custom-call | flops 2147483648 | bytes 2097152 | tf_op jit(solution)/shard_map/conv_other/pallas_call | solution.py:243
  51.0 0.0 copy-done.3
  51.0 0.0 copy-start.6
  51.0 7.8 %conv_own.1 = (f32[16,64,128]{2,1,0:T(8,128)S(1)}, bf16[64,32,128]{2,1,0:T(8,128)(2,1)}) custom-call(s32[1]{0:T(128)} %bitcast.core_ref, bf16[64,64,128]{2,1,0:T(8,128)(2,1)S(1)} %get-tuple-element.14.rows_ref, bf16[16,64,128]{2,1,0:T(8,128)(2,1)S(1)} %get-tuple-element.15.other_ref, bf16[16,8,128,128]{3,2,1,0:T(8,128)(2,1)S(1)} %copy-done.3), custom_call_target="tpu_custom_call" | custom-call | flops 2147483648 | bytes 2097152 | tf_op jit(solution)/shard_map/conv_own/pallas_call | solution.py:292
  58.8 0.0 copy-start
  58.9 0.0 copy-start.1
  58.9 7.5 %all-to-all-start.1 = ((bf16[64,32,128]{2,1,0:T(8,128)(2,1)}), bf16[64,32,128]{2,1,0:T(8,128)(2,1)S(1)}, u32[]{:S(2)}, u32[]{:S(2)}) async-start(bf16[64,32,128]{2,1,0:T(8,128)(2,1)} %get-tuple-element.17), calls=%async_computation.1 | async-start | bytes 1048576 | tf_op jit(solution)/shard_map/all_to_all | solution.py:346
  66.3 1.9 %collective-permute-start = (f32[16,64,128]{2,1,0:T(8,128)S(1)}, f32[16,64,128]{2,1,0:T(8,128)}, u32[]{:S(2)}, u32[]{:S(2)}) collective-permute-start(f32[16,64,128]{2,1,0:T(8,128)S(1)} %get-tuple-element.21), channel_id=1, source_target_pairs={{0,64},{64,0},{1,65},{65,1},{2,66},{66,2},{3,67},{67,3},{4,68},{68... | collective-permute-start | bytes 1572872 | tf_op jit(solution)/shard_map/ppermute | solution.py:344
  68.3 0.0 copy-done.6
  68.3 2.0 %multiply_convert_fusion = bf16[1,128,2048]{2,1,0:T(8,128)(2,1)} fusion(bf16[1,128,2048]{2,1,0:T(8,128)(2,1)} %param.9, bf16[1,128,2048]{2,1,0:T(8,128)(2,1)S(1)} %copy-done.6), kind=kLoop, calls=%fused_computation | loop fusion | flops 1048576 | bytes 1572864 | tf_op jit(solution)/shard_map/convert_element_type | solution.py:341
  70.3 0.0 collective-permute-done
  70.3 1.1 %add.35 = f32[16,64,128]{2,1,0:T(8,128)S(1)} add(f32[16,64,128]{2,1,0:T(8,128)S(1)} %get-tuple-element.20, f32[16,64,128]{2,1,0:T(8,128)} %collective-permute-done) | non-fusion elementwise | flops 131072 | bytes 1572864 | tf_op jit(solution)/shard_map/add | solution.py:347
  71.5 13.0 %collective-permute-start.1 = (bf16[4,64,128]{2,1,0:T(8,128)(2,1)S(1)}, bf16[4,64,128]{2,1,0:T(8,128)(2,1)S(1)}, u32[]{:S(2)}, u32[]{:S(2)}) collective-permute-start(bf16[4,64,128]{2,1,0:T(8,128)(2,1)S(1)} %get-tuple-element.24), channel_id=1, source_target_pairs={{0,256},{128,384},{256,0},{384,128},{1,257},{129,385},{257,1},{385... | collective-permute-start | bytes 196616 | tf_op jit(solution)/shard_map/ppermute | solution.py:328
  84.5 4.3 %collective-permute-start.2 = (bf16[4,64,128]{2,1,0:T(8,128)(2,1)S(1)}, bf16[4,64,128]{2,1,0:T(8,128)(2,1)S(1)}, u32[]{:S(2)}, u32[]{:S(2)}) collective-permute-start(bf16[4,64,128]{2,1,0:T(8,128)(2,1)S(1)} %get-tuple-element.23), channel_id=1, source_target_pairs={{0,128},{128,256},{256,384},{384,0},{1,129},{129,257},{257,385},{3... | collective-permute-start | bytes 196616 | tf_op jit(solution)/shard_map/ppermute | solution.py:328
  88.8 5.5 %collective-permute-start.3 = (bf16[4,64,128]{2,1,0:T(8,128)(2,1)S(1)}, bf16[4,64,128]{2,1,0:T(8,128)(2,1)S(1)}, u32[]{:S(2)}, u32[]{:S(2)}) collective-permute-start(bf16[4,64,128]{2,1,0:T(8,128)(2,1)S(1)} %get-tuple-element.22), channel_id=1, source_target_pairs={{0,384},{128,0},{256,128},{384,256},{1,385},{129,1},{257,129},{385... | collective-permute-start | bytes 196616 | tf_op jit(solution)/shard_map/ppermute | solution.py:328
  94.3 0.0 collective-permute-done.1.far_ref
  94.3 1.0 collective-permute-done.2.up_ref
  95.3 7.7 %collective-permute-done.3.down_ref = bf16[4,64,128]{2,1,0:T(8,128)(2,1)S(1)} collective-permute-done((bf16[4,64,128]{2,1,0:T(8,128)(2,1)S(1)}, bf16[4,64,128]{2,1,0:T(8,128)(2,1)S(1)}, u32[]{:S(2)}, u32[]{:S(2)}) %collective-permute-start.3) | collective-permute-done | bytes 65568 | tf_op jit(solution)/shard_map/ppermute | solution.py:328
  103.0 0.7 last_sum.1
  103.7 0.0 all-to-all-done.1.back_ref
  103.7 0.0 copy-done
  103.7 0.0 copy-done.1
  103.7 1.2 %post.1 = (bf16[128,2048]{1,0:T(8,128)(2,1)}, bf16[128,2048]{1,0:T(8,128)(2,1)}) custom-call(bf16[64,32,128]{2,1,0:T(8,128)(2,1)S(1)} %all-to-all-done.1.back_ref, bf16[128,2048]{1,0:T(8,128)(2,1)S(1)} %bitcast.19, bf16[128,2048]{1,0:T(8,128)(2,1)S(1)} %bitcast.21), custom_call_target="tpu_custom_call" | custom-call | bytes 2621440 | tf_op jit(solution)/shard_map/post/pallas_call | solution.py:58
  (2 shorter events, 0.1 us)
Async XLA Ops:
  0.6 14.4 %copy-start.7 = (bf16[32,8192]{1,0:T(8,128)(2,1)S(1)}, bf16[32,8192]{1,0:T(8,128)(2,1)}, u32[]{:S(2)}) copy-start(bf16[32,8192]{1,0:T(8,128)(2,1)} %param.11) | copy-start | bytes 1572868
  3.2 38.1 %all-to-all-start = ((bf16[64,64,128]{2,1,0:T(8,128)(2,1)}), bf16[64,64,128]{2,1,0:T(8,128)(2,1)S(1)}, u32[]{:S(2)}, u32[]{:S(2)}) async-start(bf16[64,64,128]{2,1,0:T(8,128)(2,1)} %pre.1), calls=%async_computation | async-start | bytes 2097152 | tf_op jit(solution)/shard_map/all_to_all | solution.py:340
  18.6 1.9 %copy-start.2 = (bf16[16,8,128,128]{3,2,1,0:T(8,128)(2,1)}, bf16[16,8,128,128]{3,2,1,0:T(8,128)(2,1)S(1)}, u32[]{:S(2)}) copy-start(bf16[16,8,128,128]{3,2,1,0:T(8,128)(2,1)S(1)} %get-tuple-element.16.taps_ref) | copy-start | bytes 12582916
  20.6 2.0 %copy-start.4 = (bf16[16,8,128,128]{3,2,1,0:T(8,128)(2,1)}, bf16[16,8,128,128]{3,2,1,0:T(8,128)(2,1)S(1)}, u32[]{:S(2)}) copy-start(bf16[16,8,128,128]{3,2,1,0:T(8,128)(2,1)S(1)} %get-tuple-element.13.taps_ref) | copy-start | bytes 12582916
  41.4 9.6 %copy-start.3 = (bf16[16,8,128,128]{3,2,1,0:T(8,128)(2,1)S(1)}, bf16[16,8,128,128]{3,2,1,0:T(8,128)(2,1)}, u32[]{:S(2)}) copy-start(bf16[16,8,128,128]{3,2,1,0:T(8,128)(2,1)} %copy-done.2) | copy-start | bytes 12582916
  41.4 2.3 %copy-start.5 = (bf16[16,8,128,128]{3,2,1,0:T(8,128)(2,1)S(1)}, bf16[16,8,128,128]{3,2,1,0:T(8,128)(2,1)}, u32[]{:S(2)}) copy-start(bf16[16,8,128,128]{3,2,1,0:T(8,128)(2,1)} %copy-done.4) | copy-start | bytes 12582916
  51.0 17.3 %copy-start.6 = (bf16[1,128,2048]{2,1,0:T(8,128)(2,1)S(1)}, bf16[1,128,2048]{2,1,0:T(8,128)(2,1)}, u32[]{:S(2)}) copy-start(bf16[1,128,2048]{2,1,0:T(8,128)(2,1)} %param.10) | copy-start | bytes 1572868
  58.8 44.9 %copy-start = (bf16[1,128,2048]{2,1,0:T(8,128)(2,1)S(1)}, bf16[1,128,2048]{2,1,0:T(8,128)(2,1)}, u32[]{:S(2)}) copy-start(bf16[1,128,2048]{2,1,0:T(8,128)(2,1)} %param.6) | copy-start | bytes 1572868
  58.9 44.9 %copy-start.1 = (bf16[1,128,2048]{2,1,0:T(8,128)(2,1)S(1)}, bf16[1,128,2048]{2,1,0:T(8,128)(2,1)}, u32[]{:S(2)}) copy-start(bf16[1,128,2048]{2,1,0:T(8,128)(2,1)} %param.8) | copy-start | bytes 1572868
  58.9 44.9 %all-to-all-start.1 = ((bf16[64,32,128]{2,1,0:T(8,128)(2,1)}), bf16[64,32,128]{2,1,0:T(8,128)(2,1)S(1)}, u32[]{:S(2)}, u32[]{:S(2)}) async-start(bf16[64,32,128]{2,1,0:T(8,128)(2,1)} %get-tuple-element.17), calls=%async_computation.1 | async-start | bytes 1048576 | tf_op jit(solution)/shard_map/all_to_all | solution.py:346
  66.3 4.0 %collective-permute-start = (f32[16,64,128]{2,1,0:T(8,128)S(1)}, f32[16,64,128]{2,1,0:T(8,128)}, u32[]{:S(2)}, u32[]{:S(2)}) collective-permute-start(f32[16,64,128]{2,1,0:T(8,128)S(1)} %get-tuple-element.21), channel_id=1, source_target_pairs={{0,64},{64,0},{1,65},{65,1},{2,66},{66,2},{3,67},{67,3},{4,68},{68... | collective-permute-start | bytes 1572872 | tf_op jit(solution)/shard_map/ppermute | solution.py:344
  71.5 22.8 %collective-permute-start.1 = (bf16[4,64,128]{2,1,0:T(8,128)(2,1)S(1)}, bf16[4,64,128]{2,1,0:T(8,128)(2,1)S(1)}, u32[]{:S(2)}, u32[]{:S(2)}) collective-permute-start(bf16[4,64,128]{2,1,0:T(8,128)(2,1)S(1)} %get-tuple-element.24), channel_id=1, source_target_pairs={{0,256},{128,384},{256,0},{384,128},{1,257},{129,385},{257,1},{385... | collective-permute-start | bytes 196616 | tf_op jit(solution)/shard_map/ppermute | solution.py:328
  84.5 10.8 %collective-permute-start.2 = (bf16[4,64,128]{2,1,0:T(8,128)(2,1)S(1)}, bf16[4,64,128]{2,1,0:T(8,128)(2,1)S(1)}, u32[]{:S(2)}, u32[]{:S(2)}) collective-permute-start(bf16[4,64,128]{2,1,0:T(8,128)(2,1)S(1)} %get-tuple-element.23), channel_id=1, source_target_pairs={{0,128},{128,256},{256,384},{384,0},{1,129},{129,257},{257,385},{3... | collective-permute-start | bytes 196616 | tf_op jit(solution)/shard_map/ppermute | solution.py:328
  88.8 14.2 %collective-permute-start.3 = (bf16[4,64,128]{2,1,0:T(8,128)(2,1)S(1)}, bf16[4,64,128]{2,1,0:T(8,128)(2,1)S(1)}, u32[]{:S(2)}, u32[]{:S(2)}) collective-permute-start(bf16[4,64,128]{2,1,0:T(8,128)(2,1)S(1)} %get-tuple-element.22), channel_id=1, source_target_pairs={{0,384},{128,0},{256,128},{384,256},{1,385},{129,1},{257,129},{385... | collective-permute-start | bytes 196616 | tf_op jit(solution)/shard_map/ppermute | solution.py:328
